TPU v7x, 32 devices: a whole 2x2x4 slice. The times are simulated.
32 devices in a mesh: grp: 4 (over x, core), seq: 8 (over z, y).
Axes of the slice: x: 2, y: 2, z: 4, core: 2. Of those that a mesh axis runs over, the one named last changes fastest.
Arguments:
- spans: bfloat16 [4096, 2048], P(('grp', 'seq')), may hold values from -6 to 6
- span_group: int32 [4096, 1], P(('grp', 'seq')), may hold values from 0 to 3; in each aligned block of 128 rows (0 to 127, 128 to 255, ...) at most 64 rows name the same one
- span_mask: int32 [4096], P(('grp', 'seq')), may hold values 0 or 1
- w_in: bfloat16 [2048, 1024], replicated, may hold values from -0.125 to 0.125
- norm_gain: float32 [2, 1024], replicated, may hold values from 0.25 to 1.75
- w_query: bfloat16 [2, 1024, 1024], replicated, may hold values from -8 to 8
- w_key: bfloat16 [2, 1024, 256], replicated, may hold values from -0.15625 to 0.15625
- w_value: bfloat16 [2, 1024, 256], replicated, may hold values from -0.1875 to 0.1875
- w_out: bfloat16 [2, 1024, 1024], replicated, may hold values from -0.1875 to 0.1875
- final_gain: float32 [1024], replicated, may hold values from 0.25 to 1.75
- w_class: bfloat16 [1024, 256], replicated, may hold values from -0.1875 to 0.1875
Outputs:
- hidden: bfloat16 [8192, 1024], P(('grp', 'seq'))
- logits: float32 [4, 256], P('grp')
Inputs may be any that keep to these rules, and one draw needn't show every extreme that they name: `span_group`: among the 128 spans of one device, at most 64 belong to one document; some device has exactly 64 for some document.
All inputs are finite; a program needn't handle non-finite values. No bound on the sum of `span_mask` on one device may be relied on, other than what follows from the above.
Results may differ from a plain program's by a relative error of at most 0.009.
Values may be sent and summed in bfloat16 or wider, within the bound.
No kernel may reach another device: no remote copies, remote signals or barrier semaphores. Data moves between devices by JAX's collectives and lax.ppermute only.
A program may use at most 192 MiB of HBM per device.

v0:
```python
import jax
import jax.numpy as jnp
from jax import lax
from jax.sharding import PartitionSpec as P

HEADS = 16
HDIM = 64
KV_HEADS = 4


def attend(query, keys, values, valid):
    group = HEADS // KV_HEADS
    rows = query.shape[0]
    scale = HDIM ** (-0.5)
    pieces = []
    for head in range(KV_HEADS):
        q_block = query[:, head * group * HDIM : (head + 1) * group * HDIM].reshape(
            rows, group, HDIM
        )
        k_block = keys[:, head * HDIM : (head + 1) * HDIM]
        v_block = values[:, head * HDIM : (head + 1) * HDIM]
        scores = (
            jnp.einsum("rgd,kd->rgk", q_block, k_block, preferred_element_type=jnp.float32) * scale
        )
        scores = jnp.where(valid[None, None, :] > 0, scores, -1e30)
        top = jnp.max(scores, axis=-1, keepdims=True)
        weight = jnp.exp(scores - top)
        total = jnp.sum(weight, axis=-1, keepdims=True)
        out = (
            jnp.einsum(
                "rgk,kd->rgd",
                weight.astype(jnp.bfloat16),
                v_block,
                preferred_element_type=jnp.float32,
            )
            / total
        )
        pieces.append(out.reshape(rows, group * HDIM))
    return jnp.concatenate(pieces, axis=1).astype(jnp.bfloat16)


def per_device(
    spans,
    span_group,
    span_mask,
    w_in,
    norm_gain,
    w_query,
    w_key,
    w_value,
    w_out,
    final_gain,
    w_class,
):
    rows = spans.shape[0]
    groups = lax.axis_size("grp")
    capacity = 2 * rows // groups
    slots = groups * capacity
    target = span_group[:, 0]
    member = (target[:, None] == jnp.arange(groups, dtype=jnp.int32)[None, :]).astype(jnp.int32)
    rank = jnp.sum(jnp.cumsum(member, axis=0) * member, axis=1) - 1
    slot_of = target * capacity + rank
    placing = jnp.arange(slots, dtype=jnp.int32)[:, None] == slot_of[None, :]
    valid_send = jnp.sum(jnp.where(placing, span_mask[None, :], 0), axis=1).astype(jnp.bfloat16)
    packed = jnp.dot(
        placing.astype(jnp.bfloat16), spans, preferred_element_type=jnp.float32
    ).astype(jnp.bfloat16)
    packed = packed.reshape(groups, capacity, spans.shape[1])
    arrived, live = (
        lax.all_to_all(packed, "grp", split_axis=0, concat_axis=0, tiled=True),
        lax.all_to_all(
            valid_send.reshape(groups, capacity), "grp", split_axis=0, concat_axis=0, tiled=True
        ),
    )
    arrived = arrived.reshape(slots, spans.shape[1])
    states = jnp.dot(arrived, w_in, preferred_element_type=jnp.float32).astype(jnp.bfloat16)
    valid = live.reshape(slots)
    for layer in range(w_query.shape[0]):
        xf = states.astype(jnp.float32)
        normed = (
            xf * lax.rsqrt(jnp.mean(xf * xf, axis=-1, keepdims=True) + 1e-05) * norm_gain[layer]
        ).astype(jnp.bfloat16)
        query = jnp.dot(normed, w_query[layer], preferred_element_type=jnp.float32).astype(
            jnp.bfloat16
        )
        keys_local = jnp.dot(normed, w_key[layer], preferred_element_type=jnp.float32).astype(
            jnp.bfloat16
        )
        values_local = jnp.dot(normed, w_value[layer], preferred_element_type=jnp.float32).astype(
            jnp.bfloat16
        )
        keys, values, mask_all = (
            lax.all_gather(keys_local, "seq", axis=0, tiled=True),
            lax.all_gather(values_local, "seq", axis=0, tiled=True),
            lax.all_gather(valid, "seq", axis=0, tiled=True),
        )
        attended = attend(query, keys, values, mask_all)
        states = (xf + jnp.dot(attended, w_out[layer], preferred_element_type=jnp.float32)).astype(
            jnp.bfloat16
        )
    final = states.astype(jnp.float32)
    keep = valid[:, None] > 0
    hidden = jnp.where(keep, states, jnp.zeros_like(states))
    local_sum = jnp.sum(jnp.where(keep, final, 0.0), axis=0)
    pooled = lax.psum(local_sum, "seq")
    summary = (pooled * lax.rsqrt(jnp.mean(pooled * pooled) + 1e-05) * final_gain).astype(
        jnp.bfloat16
    )
    logits = jnp.dot(summary[None, :], w_class, preferred_element_type=jnp.float32)
    return (hidden, logits)


def solution(mesh):
    return jax.shard_map(
        per_device,
        mesh=mesh,
        in_specs=(
            P(("grp", "seq"), None),
            P(("grp", "seq"), None),
            P(("grp", "seq")),
            P(),
            P(),
            P(),
            P(),
            P(),
            P(),
            P(),
            P(),
        ),
        out_specs=(P(("grp", "seq"), None), P("grp", None)),
        check_vma=False,
    )
```

profile of v0, /device:TPU:0, one launch (start us, length us, event | category | flops | bytes accessed | tf_op | source)
XLA Modules:
  0.0 255.3 jit_solution(17939923890507356619)
XLA Ops:
  9.7 1.4 convolution_convert_fusion
  11.1 4.2 %all-to-all-start.1 = ((bf16[4,64,2048]{2,1,0:T(8,128)(2,1)}), bf16[4,64,2048]{2,1,0:T(8,128)(2,1)S(1)}, u32[]{:S(2)}, u32[]{:S(2)}) async-start(bf16[4,64,2048]{2,1,0:T(8,128)(2,1)} %bitcast.1), calls=%async_computation.1 | async-start | bytes 2097152 | tf_op jit(solution)/shard_map/all_to_all | solution.py:70
  16.1 13.7 %all-to-all-done.1 = bf16[4,64,2048]{2,1,0:T(8,128)(2,1)S(1)} async-done(((bf16[4,64,2048]{2,1,0:T(8,128)(2,1)}), bf16[4,64,2048]{2,1,0:T(8,128)(2,1)S(1)}, u32[]{:S(2)}, u32[]{:S(2)}) %all-to-all-start.1) | async-done | bytes 1048608 | tf_op jit(solution)/shard_map/all_to_all | solution.py:70
  29.8 3.5 %fusion.124 = (f32[256]{0:T(256)S(1)}, bf16[256,1024]{1,0:T(8,128)(2,1)S(1)}) fusion(bf16[256,2048]{1,0:T(8,128)(2,1)S(1)} %bitcast.138, bf16[2048,1024]{1,0:T(8,128)(2,1)} %param.14), kind=kOutput, calls=%fused_computation.100 | convolution fusion | flops 1074790144 | bytes 5768192 | tf_op jit(solution)/shard_map/dot_general | solution.py:76
  34.7 6.1 %all_to_all.11 = bf16[4,1,64]{2,1,0:T(2,128)(2,1)S(1)} all-to-all(bf16[4,1,64]{2,1,0:T(2,128)(2,1)S(1)} %convert_element_type.119), channel_id=1, replica_groups=mesh['grp'=4,'seq'=8] {'grp'}, dimensions={0} | all-to-all | bytes 1024 | tf_op jit(solution)/shard_map/all_to_all | solution.py:71
  40.9 21.5 %all-gather = bf16[8,1,256]{2,1,0:T(2,128)(2,1)S(1)} all-gather(bf16[1,1,256]{2,1,0:T(2,128)(2,1)S(1)} %reshape.156), channel_id=1, replica_groups=mesh['grp'=4,'seq'=8] {'seq'}, dimensions={0}, use_global_device_ids=true | all-gather | bytes 4608 | tf_op jit(solution)/shard_map/all_gather | solution.py:95
  62.5 2.4 fusion.70
  65.3 2.1 convolution_convert_fusion.4
  68.0 7.9 %all-gather.6.cloned.1.call-done = bf16[2048,256]{1,0:T(8,128)(2,1)} async-done(((bf16[256,256]{1,0:T(8,128)(2,1)}), bf16[2048,256]{1,0:T(8,128)(2,1)}) %all-gather.6.cloned.1.call-update) | async-done | bytes 1048592 | tf_op jit(solution)/shard_map/all_gather | solution.py:93
  75.8 2.5 fusion.134
  79.6 5.2 %fusion = (f32[256,4]{0,1:T(4,128)S(1)}, f32[256,4,2048]{2,0,1:T(8,128)}) fusion(pred[2048]{0:T(1024)(128)(4,1)S(1)} %reshape.159, bf16[256,4,64]{0,2,1:T(8,128)(2,1)S(1)} %bitcast.139, bf16[2048,256]{1,0:T(8,128)(2,1)S(1)} %copy-done.9), kind=kOutput, calls=%fused_computation.16 | convolution fusion | flops 274725888 | bytes 9050112 | tf_op jit(solution)/shard_map/rgd,kd->rgk/dot_general | solution.py:23
  84.9 10.9 %fusion.8 = (f32[256,4]{0,1:T(4,128)S(1)}, f32[256,4]{0,1:T(4,128)S(1)}, f32[256,4]{0,1:T(4,128)S(1)}, f32[256,4]{0,1:T(4,128)S(1)}, f32[256,4,2048]{2,0,1:T(8,128)}) fusion(f32[256,4,2048]{2,0,1:T(8,128)} %get-tuple-element.29, f32[256,4]{0,1:T(4,128)S(1)} %get-tuple-element.28, pred[2048]{0:T(1024)(128)(4,1)S(1)} %reshape.159, ...), kind=kOutput, calls=%fused_computation.24 | convolution fusion | flops 295694336 | bytes 34232320 | tf_op jit(solution)/shard_map/rgd,kd->rgk/dot_general | solution.py:23
  95.8 7.5 %fusion.10 = (f32[256,4]{0,1:T(4,128)S(1)}, f32[256,4]{0,1:T(4,128)S(1)}, f32[256,4]{0,1:T(4,128)S(1)}) fusion(f32[256,4,2048]{2,0,1:T(8,128)} %get-tuple-element.30, f32[256,4]{0,1:T(4,128)S(1)} %get-tuple-element.10, pred[2048]{0:T(1024)(128)(4,1)S(1)} %reshape.159, f32[256,4]{0,1:T(4,128)S(1)} %get-tuple-element.11, f32[256,4,2048]{2,0,1:T(8,128)S(1)} %fusion.135, ...), kind=kLoop, calls=%fused_computation.26 | loop fusion | flops 25162752 | bytes 25192448 | tf_op jit(solution)/shard_map/reduce_sum | solution.py:28
  103.4 13.5 %all-gather.8.cloned.1.call-done = bf16[2048,256]{1,0:T(8,128)(2,1)} async-done(((bf16[256,256]{1,0:T(8,128)(2,1)}), bf16[2048,256]{1,0:T(8,128)(2,1)}) %all-gather.8.cloned.1.call-update) | async-done | bytes 1048592 | tf_op jit(solution)/shard_map/all_gather | solution.py:94
  116.9 5.4 %fusion.97 = bf16[256,4,64]{0,2,1:T(8,128)(2,1)S(1)} fusion(f32[256,4,2048]{2,0,1:T(8,128)} %copy-done.4, f32[256,4]{0,1:T(4,128)S(1)} %get-tuple-element.12, pred[2048]{0:T(1024)(128)(4,1)S(1)} %reshape.159, bf16[2048,256]{1,0:T(8,128)(2,1)} %all-gather.8.cloned.1.call-done, f32[256,4]{0,1:T(4,128)S(1)} %get-tuple-element.15), kind=kOutput, calls=%fused_computation.91 | convolution fusion | flops 276955136 | bytes 9054208 | tf_op jit(solution)/shard_map/rgk,kd->rgd/dot_general | solution.py:30
  123.0 1.9 fusion.91
  125.8 1.9 fusion.85
  128.2 1.9 fusion.79
  132.4 2.3 fusion.73
  135.2 2.1 convolution_convert_fusion.2
  137.3 33.8 %all-gather.10.cloned.1.call-done = bf16[2048,256]{1,0:T(8,128)(2,1)} async-done(((bf16[256,256]{1,0:T(8,128)(2,1)}), bf16[2048,256]{1,0:T(8,128)(2,1)}) %all-gather.10.cloned.1.call-update) | async-done | bytes 1048592 | tf_op jit(solution)/shard_map/all_gather | solution.py:93
  171.1 2.5 fusion.130
  173.6 5.0 %fusion.4 = (f32[256,4]{0,1:T(4,128)S(1)}, f32[256,4,2048]{2,0,1:T(8,128)}) fusion(pred[2048]{0:T(1024)(128)(4,1)S(1)} %reshape.159, bf16[256,4,64]{0,2,1:T(8,128)(2,1)S(1)} %bitcast.141, bf16[2048,256]{1,0:T(8,128)(2,1)S(1)} %copy-done.10), kind=kOutput, calls=%fused_computation.20 | convolution fusion | flops 274725888 | bytes 9050112 | tf_op jit(solution)/shard_map/rgd,kd->rgk/dot_general | solution.py:23
  179.9 12.4 %fusion.16 = (f32[256,4]{0,1:T(4,128)S(1)}, f32[256,4]{0,1:T(4,128)S(1)}, f32[256,4]{0,1:T(4,128)S(1)}, f32[256,4]{0,1:T(4,128)S(1)}, f32[256,4,2048]{2,0,1:T(8,128)}) fusion(f32[256,4,2048]{2,0,1:T(8,128)} %get-tuple-element.34, f32[256,4]{0,1:T(4,128)S(1)} %get-tuple-element.33, pred[2048]{0:T(1024)(128)(4,1)S(1)} %reshape.159, ...), kind=kOutput, calls=%fused_computation.32 | convolution fusion | flops 295694336 | bytes 34232320 | tf_op jit(solution)/shard_map/rgd,kd->rgk/dot_general | solution.py:23
  192.4 7.6 %fusion.18 = (f32[256,4]{0,1:T(4,128)S(1)}, f32[256,4]{0,1:T(4,128)S(1)}, f32[256,4]{0,1:T(4,128)S(1)}) fusion(f32[256,4,2048]{2,0,1:T(8,128)} %get-tuple-element.35, f32[256,4]{0,1:T(4,128)S(1)} %get-tuple-element.3, pred[2048]{0:T(1024)(128)(4,1)S(1)} %reshape.159, f32[256,4]{0,1:T(4,128)S(1)} %get-tuple-element.4, f32[256,4,2048]{2,0,1:T(8,128)S(1)} %fusion.131, ...), kind=kLoop, calls=%fused_computation.34 | loop fusion | flops 25162752 | bytes 25192448 | tf_op jit(solution)/shard_map/reduce_sum | solution.py:28
  200.0 12.0 %all-gather.12.cloned.1.call-done = bf16[2048,256]{1,0:T(8,128)(2,1)} async-done(((bf16[256,256]{1,0:T(8,128)(2,1)}), bf16[2048,256]{1,0:T(8,128)(2,1)}) %all-gather.12.cloned.1.call-update) | async-done | bytes 1048592 | tf_op jit(solution)/shard_map/all_gather | solution.py:94
  212.0 5.4 %fusion.121 = bf16[256,4,64]{0,2,1:T(8,128)(2,1)S(1)} fusion(f32[256,4,2048]{2,0,1:T(8,128)} %copy-done.5, f32[256,4]{0,1:T(4,128)S(1)} %get-tuple-element.5, pred[2048]{0:T(1024)(128)(4,1)S(1)} %reshape.159, bf16[2048,256]{1,0:T(8,128)(2,1)} %all-gather.12.cloned.1.call-done, f32[256,4]{0,1:T(4,128)S(1)} %get-tuple-element.8), kind=kOutput, calls=%fused_computation.99 | convolution fusion | flops 276955136 | bytes 9054208 | tf_op jit(solution)/shard_map/rgk,kd->rgd/dot_general | solution.py:30
  218.2 1.9 fusion.115
  221.0 1.9 fusion.109
  223.5 1.9 fusion.103
  225.5 1.5 broadcast_select_fusion
  227.2 19.2 %psum.7 = f32[1024]{0:T(1024)S(1)} all-reduce(f32[1024]{0:T(1024)S(1)} %select_reduce_fusion), channel_id=1, replica_groups=mesh['grp'=4,'seq'=8] {'seq'}, use_global_device_ids=true, to_apply=%region_22.23 | all-reduce | flops 1024 | bytes 8192 | tf_op jit(solution)/shard_map/psum | solution.py:105
  (107 shorter events, 17.1 us)
Async XLA Ops:
  7.2 2.6 %copy-start = (bf16[128,2048]{1,0:T(8,128)(2,1)S(1)}, bf16[128,2048]{1,0:T(8,128)(2,1)}, u32[]{:S(2)}) copy-start(bf16[128,2048]{1,0:T(8,128)(2,1)} %param.11) | copy-start | bytes 1572868
  7.2 26.2 %copy-start.16 = (bf16[2,1024,256]{2,1,0:T(8,128)(2,1)S(1)}, bf16[2,1024,256]{2,1,0:T(8,128)(2,1)}, u32[]{:S(2)}) copy-start(bf16[2,1024,256]{2,1,0:T(8,128)(2,1)} %param.17) | copy-start | bytes 3145732
  7.2 27.3 %copy-start.13 = (s32[128]{0:T(128)S(1)}, s32[128]{0:T(128)}, u32[]{:S(2)}) copy-start(s32[128]{0:T(128)} %param.13) | copy-start | bytes 1540
  11.1 18.7 %all-to-all-start.1 = ((bf16[4,64,2048]{2,1,0:T(8,128)(2,1)}), bf16[4,64,2048]{2,1,0:T(8,128)(2,1)S(1)}, u32[]{:S(2)}, u32[]{:S(2)}) async-start(bf16[4,64,2048]{2,1,0:T(8,128)(2,1)} %bitcast.1), calls=%async_computation.1 | async-start | bytes 2097152 | tf_op jit(solution)/shard_map/all_to_all | solution.py:70
  15.4 60.5 %all-gather.6.cloned.1.call-start = ((), (), s32[]{:S(2)}) async-start(), calls=%async_computation.2 | async-start | bytes 1179648 | tf_op jit(solution)/shard_map/all_gather | solution.py:93
  33.3 34.6 %copy-start.20 = (bf16[256,1024]{1,0:T(8,128)(2,1)}, bf16[256,1024]{1,0:T(8,128)(2,1)S(1)}, u32[]{:S(2)}) copy-start(bf16[256,1024]{1,0:T(8,128)(2,1)S(1)} %get-tuple-element.27) | copy-start | bytes 1572868
  34.4 82.5 %all-gather.8.cloned.1.call-start = ((), (), s32[]{:S(2)}) async-start(), calls=%async_computation.3 | async-start | bytes 1179648 | tf_op jit(solution)/shard_map/all_gather | solution.py:94
  67.4 103.7 %all-gather.10.cloned.1.call-start = ((), (), s32[]{:S(2)}) async-start(), calls=%async_computation.4 | async-start | bytes 1179648 | tf_op jit(solution)/shard_map/all_gather | solution.py:93
  75.8 2.5 copy-start.9
  78.3 17.5 %copy-start.4 = (f32[256,4,2048]{2,0,1:T(8,128)}, f32[256,4,2048]{2,0,1:T(8,128)S(1)}, u32[]{:S(2)}) copy-start(f32[256,4,2048]{2,0,1:T(8,128)S(1)} %fusion.134) | copy-start | bytes 25165828
  79.6 16.2 %copy-start.2 = (f32[256,4,2048]{2,0,1:T(8,128)}, f32[256,4,2048]{2,0,1:T(8,128)S(1)}, u32[]{:S(2)}) copy-start(f32[256,4,2048]{2,0,1:T(8,128)S(1)} %fusion.135) | copy-start | bytes 25165828
  116.9 5.9 %copy-start.3 = (f32[256,4,2048]{2,0,1:T(8,128)S(1)}, f32[256,4,2048]{2,0,1:T(8,128)}, u32[]{:S(2)}) copy-start(f32[256,4,2048]{2,0,1:T(8,128)} %copy-done.2) | copy-start | bytes 25165828
  116.9 6.1 %copy-start.18 = (bf16[2048,256]{1,0:T(8,128)(2,1)S(1)}, bf16[2048,256]{1,0:T(8,128)(2,1)}, u32[]{:S(2)}) copy-start(bf16[2048,256]{1,0:T(8,128)(2,1)} %all-gather.8.cloned.1.call-done) | copy-start | bytes 3145732
  116.9 8.0 %slice-start.4 = ((s8[8388608]{0:T(1024)(128)(4,1)}), s8[4194304]{0:T(1024)(128)(4,1)S(1)}, s32[]{:S(2)}) async-start(s8[8388608]{0:T(1024)(128)(4,1)} %bitcast.136), calls=%async_computation.10 | async-start | bytes 8388608
  122.3 3.4 %slice-start.5 = ((s8[8388608]{0:T(1024)(128)(4,1)}), s8[4194304]{0:T(1024)(128)(4,1)S(1)}, s32[]{:S(2)}) async-start(s8[8388608]{0:T(1024)(128)(4,1)} %bitcast.136), calls=%async_computation.11 | async-start | bytes 8388608
  123.0 4.6 %slice-start.2 = ((s8[8388608]{0:T(1024)(128)(4,1)}), s8[4194304]{0:T(1024)(128)(4,1)S(1)}, s32[]{:S(2)}) async-start(s8[8388608]{0:T(1024)(128)(4,1)} %bitcast.134), calls=%async_computation.8 | async-start | bytes 8388608
  125.7 2.4 slice-start.3
  130.0 5.1 %copy-start.17 = (bf16[2,1024,256]{2,1,0:T(8,128)(2,1)S(1)}, bf16[2,1024,256]{2,1,0:T(8,128)(2,1)}, u32[]{:S(2)}) copy-start(bf16[2,1024,256]{2,1,0:T(8,128)(2,1)} %param.18) | copy-start | bytes 3145732
  132.0 80.0 %all-gather.12.cloned.1.call-start = ((), (), s32[]{:S(2)}) async-start(), calls=%async_computation.5 | async-start | bytes 1179648 | tf_op jit(solution)/shard_map/all_gather | solution.py:94
  171.1 2.5 copy-start.10
  173.6 18.8 %copy-start.5 = (f32[256,4,2048]{2,0,1:T(8,128)}, f32[256,4,2048]{2,0,1:T(8,128)S(1)}, u32[]{:S(2)}) copy-start(f32[256,4,2048]{2,0,1:T(8,128)S(1)} %fusion.130) | copy-start | bytes 25165828
  179.9 12.4 %copy-start.6 = (f32[256,4,2048]{2,0,1:T(8,128)}, f32[256,4,2048]{2,0,1:T(8,128)S(1)}, u32[]{:S(2)}) copy-start(f32[256,4,2048]{2,0,1:T(8,128)S(1)} %fusion.131) | copy-start | bytes 25165828
  212.0 5.9 %copy-start.7 = (f32[256,4,2048]{2,0,1:T(8,128)S(1)}, f32[256,4,2048]{2,0,1:T(8,128)}, u32[]{:S(2)}) copy-start(f32[256,4,2048]{2,0,1:T(8,128)} %copy-done.6) | copy-start | bytes 25165828
  212.0 6.1 %copy-start.19 = (bf16[2048,256]{1,0:T(8,128)(2,1)S(1)}, bf16[2048,256]{1,0:T(8,128)(2,1)}, u32[]{:S(2)}) copy-start(bf16[2048,256]{1,0:T(8,128)(2,1)} %all-gather.12.cloned.1.call-done) | copy-start | bytes 3145732
  217.4 3.6 %copy-start.8 = (f32[256,4,2048]{2,0,1:T(8,128)S(1)}, f32[256,4,2048]{2,0,1:T(8,128)}, u32[]{:S(2)}) copy-start(f32[256,4,2048]{2,0,1:T(8,128)} %get-tuple-element.35) | copy-start | bytes 25165828
  218.2 4.8 %slice-start = ((s8[8388608]{0:T(1024)(128)(4,1)}), s8[4194304]{0:T(1024)(128)(4,1)S(1)}, s32[]{:S(2)}) async-start(s8[8388608]{0:T(1024)(128)(4,1)} %bitcast.132), calls=%async_computation.6 | async-start | bytes 8388608
  221.0 2.4 slice-start.1
  222.9 2.5 copy-start.15
  222.9 2.5 copy-start.23
  222.9 25.5 %copy-start.1 = (bf16[128,2048]{1,0:T(8,128)(2,1)S(1)}, bf16[128,2048]{1,0:T(8,128)(2,1)}, u32[]{:S(2)}) copy-start(bf16[128,2048]{1,0:T(8,128)(2,1)} %param.11) | copy-start | bytes 1572868
  223.5 24.2 %copy-start.12 = (f32[1024]{0:T(1024)S(1)}, f32[1024]{0:T(1024)}, u32[]{:S(2)}) copy-start(f32[1024]{0:T(1024)} %param.20) | copy-start | bytes 12292
  223.5 24.3 %copy-start.11 = (bf16[1024,256]{1,0:T(8,128)(2,1)S(1)}, bf16[1024,256]{1,0:T(8,128)(2,1)}, u32[]{:S(2)}) copy-start(bf16[1024,256]{1,0:T(8,128)(2,1)} %param.21) | copy-start | bytes 1572868
  (3 other events, 6.2 us)
Sparse Core Ops, SparseCore 0:
  34.5 41.2 all-gather.5
  78.0 38.8 all-gather.7
  132.1 38.9 all-gather.9
  173.1 38.8 all-gather.11
where the time goes:
time: 259 us; the launch traced here: 255 us
  matrix products  82.1 us (32%)
  waiting for transfers between devices  81 us (31%)
  blocking collectives  46.8 us (18%)
  other arithmetic  18.7 us (7%)
  between operations  15.2 us (6%)
  local copies, waits for them, and re-layouts  6.44 us (2%)
  starting transfers between devices  5.07 us (2%)
    all_gather x2, waiting for transfers between devices, per_device(): lax.all_gather(keys_local, 'seq', axis=0, tiled=True)  41.7 us
    dot_general x8, matrix products, attend(): jnp.einsum('rgd,kd->rgk', q_block, k_block, preferred_element_type=jnp.fl...  41.1 us
    all_gather x2, waiting for transfers between devices, per_device(): lax.all_gather(values_local, 'seq', axis=0, tiled=True)  25.6 us
    dot_general x8, matrix products, attend(): jnp.einsum('rgk,kd->rgd', weight.astype(jnp.bfloat16), v_block, preferred...  22.1 us
    all_gather x1, blocking collectives, per_device(): lax.all_gather(valid, 'seq', axis=0, tiled=True)  21.5 us
    psum x1, blocking collectives, per_device(): pooled = lax.psum(local_sum, 'seq')  19.2 us
    reduce_sum x2, other arithmetic, attend(): total = jnp.sum(weight, axis=-1, keepdims=True)  15.2 us
    all_to_all x1, waiting for transfers between devices, per_device(): lax.all_to_all(packed, 'grp', split_axis=0, concat_axis=0, tiled=True)  13.7 us
  transfers between devices with their start and end apart: 5, of which 5 were waited for; matrix products, arithmetic and copies ran while one was open for 26% of the time, Pallas kernels for 0%

commit v1 on v0

v1 whole, which is shorter than its diff:
```python
import functools

import jax
import jax.numpy as jnp
from jax import lax
from jax.experimental import pallas as pl
from jax.experimental.pallas import tpu as pltpu
from jax.sharding import PartitionSpec as P

HEADS = 16
HDIM = 64
KV_HEADS = 4
KV = KV_HEADS * HDIM
LANES = 128
EXTRA = 8
FAR = -1e30


def attend_kernel(stacked, carried, last, *refs):
    count = len(stacked)
    q_ref, doc_ref, far_ref = refs[:3]
    blocks = refs[3 : 3 + count]
    refs = refs[3 + count :]
    if carried:
        acc_in, stat_in = refs[:2]
        refs = refs[2:]
    if last:
        out_ref, ka, va = refs
    else:
        acc_out, stat_out, ka, va = refs
    rows = q_ref.shape[0]
    lane = lax.broadcasted_iota(jnp.int32, (rows, LANES), 1)
    low = lane < HDIM
    ka[:, LANES:] = far_ref[...]
    va[:, LANES:] = jnp.ones((va.shape[0], LANES), jnp.bfloat16)
    stats = jnp.zeros((rows, LANES), jnp.float32)
    doc = doc_ref[...]
    for pair in range(KV_HEADS // 2):
        at = 0
        for block, number in zip(blocks, stacked):
            for i in range(max(number, 1)):
                view = block.at[i] if number else block
                ka[at : at + rows, :LANES] = view[:rows, pair * LANES : (pair + 1) * LANES]
                va[at : at + rows, :LANES] = view[
                    :rows, KV + pair * LANES : KV + (pair + 1) * LANES
                ]
                at += rows
        for step in range(HEADS // 4):
            head = pair * (HEADS // 2) + 2 * step
            upper = head // (HEADS // KV_HEADS) % 2
            columns = slice(head * HDIM, head * HDIM + LANES)
            both = q_ref[:, columns].astype(jnp.float32)
            turned = pltpu.roll(both, HDIM, 1)
            first, second = (turned, both) if upper else (both, turned)
            keep = ~low if upper else low
            first = jnp.where(keep, first, 0.0).astype(jnp.bfloat16)
            second = jnp.where(keep, second, 0.0).astype(jnp.bfloat16)
            queries = jnp.concatenate(
                [jnp.concatenate([first, doc], 1), jnp.concatenate([second, doc], 1)], 0
            )
            scores = lax.dot_general(
                queries, ka[...], (((1,), (1,)), ((), ())), preferred_element_type=jnp.float32
            )
            top = jnp.max(scores, axis=1, keepdims=True)
            if carried:
                before = jnp.concatenate(
                    [stat_in[:, head : head + 1], stat_in[:, head + 1 : head + 2]], 0
                )
                top = jnp.maximum(top, before)
                shrink = jnp.exp(before - top)
            weight = jnp.exp(scores - top).astype(jnp.bfloat16)
            product = jnp.dot(weight, va[...], preferred_element_type=jnp.float32)
            total = product[:, LANES:]
            if upper:
                block = jnp.where(low, pltpu.roll(product[:rows, :LANES], HDIM, 1), product[rows:, :LANES])
            else:
                block = jnp.where(low, product[:rows, :LANES], pltpu.roll(product[rows:, :LANES], HDIM, 1))
            total = jnp.where(low, total[:rows], total[rows:])
            if carried:
                factor = jnp.where(low, shrink[:rows], shrink[rows:])
                block = block + factor * acc_in[:, columns]
                old = jnp.where(
                    low,
                    stat_in[:, HDIM + head : HDIM + head + 1],
                    stat_in[:, HDIM + head + 1 : HDIM + head + 2],
                )
                total = total + factor * old
            if last:
                out_ref[:, columns] = (block / total).astype(jnp.bfloat16)
            else:
                acc_out[:, columns] = block
                stats = jnp.where(lane == head, top[:rows], stats)
                stats = jnp.where(lane == head + 1, top[rows:], stats)
                stats = jnp.where(lane == HDIM + head, total[:, :1], stats)
                stats = jnp.where(lane == HDIM + head + 1, total[:, HDIM : HDIM + 1], stats)
    if not last:
        stat_out[...] = stats


def attend(query, doc, far, blocks, carry, last):
    rows, width = query.shape
    stacked = tuple(b.shape[0] if b.ndim == 3 else 0 for b in blocks)
    keys = rows * sum(max(n, 1) for n in stacked)
    if last:
        out = jax.ShapeDtypeStruct((rows, width), jnp.bfloat16)
    else:
        out = (
            jax.ShapeDtypeStruct((rows, width), jnp.float32),
            jax.ShapeDtypeStruct((rows, LANES), jnp.float32),
        )
    carried = () if carry is None else carry
    return pl.pallas_call(
        functools.partial(attend_kernel, stacked, carry is not None, last),
        out_shape=out,
        scratch_shapes=[
            pltpu.VMEM((keys, 2 * LANES), jnp.bfloat16),
            pltpu.VMEM((keys, 2 * LANES), jnp.bfloat16),
        ],
        compiler_params=pltpu.CompilerParams(vmem_limit_bytes=56 * 1024 * 1024),
        cost_estimate=pl.CostEstimate(
            flops=4 * rows * keys * width,
            bytes_accessed=keys * 4 * KV,
            transcendentals=rows * keys * HEADS,
        ),
        name="attend",
    )(query, doc, far, *blocks, *carried)


def across(array, axis, bit):
    size = lax.axis_size(axis)
    return lax.ppermute(array, axis, [(i, i ^ bit) for i in range(size)])


def gather_blocks(block):
    grp, seq = lax.axis_size("grp"), lax.axis_size("seq")
    if (grp, seq) != (4, 8):
        whole = lax.all_gather(block, ("grp", "seq"), axis=0, tiled=False)
        part = 32 if whole.shape[0] % 32 == 0 else whole.shape[0]
        return [[whole[i : i + part]] for i in range(0, whole.shape[0], part)]
    line = [block] + [across(block, "seq", bit) for bit in (2, 4, 6)]
    side = [across(b, "grp", 2) for b in line]
    flat = [across(b, "seq", 1) for b in line]
    corner = [across(b, "grp", 2) for b in flat[:2]] + [across(b, "seq", 1) for b in side[2:]]
    groups = (line, side, flat, corner)
    other = [across(jnp.stack(g), "grp", 1) for g in groups]
    return [[b for g in groups for b in g] + other]


def placement(code, lanes):
    return jnp.where(code[:, None] == lanes[None, :], 0.0, FAR).astype(jnp.bfloat16)


def per_device(
    spans,
    span_group,
    span_mask,
    w_in,
    norm_gain,
    w_query,
    w_key,
    w_value,
    w_out,
    final_gain,
    w_class,
):
    rows = spans.shape[0]
    groups = lax.axis_size("grp")
    capacity = 2 * rows // groups
    slots = groups * capacity
    target = span_group[:, 0]
    number = jnp.arange(rows, dtype=jnp.int32)
    earlier = (number[None, :] < number[:, None]) & (target[None, :] == target[:, None])
    rank = jnp.sum(earlier.astype(jnp.int32), axis=1)
    slot_of = target * capacity + rank
    placing = (jnp.arange(slots, dtype=jnp.int32)[:, None] == slot_of[None, :]) & (
        span_mask[None, :] > 0
    )
    placing = placing.astype(jnp.bfloat16)
    lanes = jnp.arange(LANES, dtype=jnp.int32)
    doc = (target[:, None] == lanes[None, :]).astype(jnp.bfloat16)
    code = jnp.where(span_mask > 0, target, LANES).astype(jnp.bfloat16)
    states = jnp.dot(spans, w_in, preferred_element_type=jnp.float32).astype(jnp.bfloat16)
    far = None
    for layer in range(w_query.shape[0]):
        xf = states.astype(jnp.float32)
        normed = (
            xf * lax.rsqrt(jnp.mean(xf * xf, axis=-1, keepdims=True) + 1e-05) * norm_gain[layer]
        ).astype(jnp.bfloat16)
        keys = jnp.dot(normed, w_key[layer], preferred_element_type=jnp.float32)
        values = jnp.dot(normed, w_value[layer], preferred_element_type=jnp.float32)
        block = jnp.concatenate([keys, values], axis=1).astype(jnp.bfloat16)
        if layer == 0:
            tail = jnp.broadcast_to(jnp.pad(code, (0, 2 * KV - rows))[None, :], (EXTRA, 2 * KV))
            block = jnp.concatenate([block, tail], axis=0)
        query = jnp.dot(normed, w_query[layer], preferred_element_type=jnp.float32).astype(
            jnp.bfloat16
        )
        query = query * jnp.bfloat16(HDIM**-0.5)
        stages = gather_blocks(block)
        if far is None:
            far = []
            for stage in stages:
                codes = [
                    b[..., rows, :rows].reshape(-1) for b in stage
                ]
                far.append(placement(jnp.concatenate(codes).astype(jnp.int32), lanes))
        carry = None
        for i, stage in enumerate(stages):
            carry = attend(query, doc, far[i], stage, carry, i == len(stages) - 1)
        states = (xf + jnp.dot(carry, w_out[layer], preferred_element_type=jnp.float32)).astype(
            jnp.bfloat16
        )
    packed = jnp.dot(placing, states, preferred_element_type=jnp.float32).astype(jnp.bfloat16)
    packed = packed.reshape(groups, capacity, states.shape[1])
    hidden = lax.all_to_all(packed, "grp", split_axis=0, concat_axis=0, tiled=True)
    hidden = hidden.reshape(slots, states.shape[1])
    local_sum = jnp.sum(hidden.astype(jnp.float32), axis=0)
    size = lax.axis_size("seq")
    sums = lax.all_to_all(
        jnp.broadcast_to(local_sum[None, :], (size, local_sum.shape[0])),
        "seq",
        split_axis=0,
        concat_axis=0,
        tiled=True,
    )
    pooled = jnp.sum(sums, axis=0)
    summary = (pooled * lax.rsqrt(jnp.mean(pooled * pooled) + 1e-05) * final_gain).astype(
        jnp.bfloat16
    )
    logits = jnp.dot(summary[None, :], w_class, preferred_element_type=jnp.float32)
    return (hidden, logits)


def solution(mesh):
    return jax.shard_map(
        per_device,
        mesh=mesh,
        in_specs=(
            P(("grp", "seq"), None),
            P(("grp", "seq"), None),
            P(("grp", "seq")),
            P(),
            P(),
            P(),
            P(),
            P(),
            P(),
            P(),
            P(),
        ),
        out_specs=(P(("grp", "seq"), None), P("grp", None)),
        check_vma=False,
    )
```

time: 259 us -> 182 us (0.70); the launches traced: 255 us -> 181 us
  matrix products: 82.1 us -> 12.8 us
  waiting for transfers between devices: 81 us -> 23.9 us
  starting transfers between devices: 5.07 us -> 46.6 us
  local copies, waits for them, and re-layouts: 6.44 us -> 45.6 us
  blocking collectives: 46.8 us -> 11.2 us
  Pallas kernels: 0 us -> 30.3 us
  between operations: 15.2 us -> 2.06 us
  other arithmetic: 18.7 us -> 8.39 us
    dot_general x24 -> x7, matrix products: 76.7 us -> 8.17 us  [the longest x1 2.98 us: per_device(): jnp.dot(spans, w_in, preferred_element_type=jnp.float32)]
    all_gather x4 -> x0, waiting for transfers between devices: 67.3 us -> none  [the longest x2 41.7 us: per_device(): lax.all_gather(keys_local, 'seq', axis=0, tiled=True)]
    ppermute x0 -> x38, starting transfers between devices: none -> 42.4 us  [across(): return lax.ppermute(array, axis, [(i, i ^ bit) for i in range(size)])]
    pallas_call x0 -> x2, Pallas kernels: none -> 30.3 us  [attend(): pl.pallas_call(functools.partial(attend_kernel, stacked, carry is not Non...]
    unnamed x61 -> x110, local copies, waits for them, and re-layouts: 4.6 us -> 30.2 us
    all_gather x1 -> x0, blocking collectives: 21.5 us -> none  [per_device(): lax.all_gather(valid, 'seq', axis=0, tiled=True)]
    psum x1 -> x0, blocking collectives: 19.2 us -> none  [per_device(): pooled = lax.psum(local_sum, 'seq')]
    ppermute x0 -> x38, waiting for transfers between devices: none -> 17.2 us  [across(): return lax.ppermute(array, axis, [(i, i ^ bit) for i in range(size)])]
  transfers between devices with their start and end apart: 5 -> 39, of which waited for: 5 -> 12; matrix products, arithmetic and copies ran while one was open for 26% -> 26% of each run, Pallas kernels for 0% -> 0%
where the time goes in v1:
time: 182 us; the launch traced here: 181 us
  starting transfers between devices  46.6 us (26%)
  local copies, waits for them, and re-layouts  45.6 us (25%)
  Pallas kernels  30.3 us (17%)
  waiting for transfers between devices  23.9 us (13%)
  matrix products  12.8 us (7%)
  blocking collectives  11.2 us (6%)
  other arithmetic  8.39 us (5%)
  between operations  2.06 us (1%)
    ppermute x38, starting transfers between devices, across(): return lax.ppermute(array, axis, [(i, i ^ bit) for i in range(size)])  42.4 us
    pallas_call x2, Pallas kernels, attend(): pl.pallas_call(functools.partial(attend_kernel, stacked, carry is not Non...  30.3 us
    unnamed x110, local copies, waits for them, and re-layouts  30.2 us
    ppermute x38, waiting for transfers between devices, across(): return lax.ppermute(array, axis, [(i, i ^ bit) for i in range(size)])  17.2 us
    concatenate x16, local copies, waits for them, and re-layouts, per_device(): far.append(placement(jnp.concatenate(codes).astype(jnp.int32), lanes))  11.3 us
    all_to_all x1, blocking collectives, per_device(): lax.all_to_all(packed, 'grp', split_axis=0, concat_axis=0, tiled=True)  11.2 us
    all_to_all x1, waiting for transfers between devices, per_device(): lax.all_to_all(jnp.broadcast_to(local_sum[None, :], (size, local_sum.shap...  6.69 us
    all_to_all x1, starting transfers between devices, per_device(): lax.all_to_all(jnp.broadcast_to(local_sum[None, :], (size, local_sum.shap...  4.22 us
  transfers between devices with their start and end apart: 39, of which 12 were waited for; matrix products, arithmetic and copies ran while one was open for 26% of the time, Pallas kernels for 0%

profile of v1, /device:TPU:0, one launch (start us, length us, event | category | flops | bytes accessed | tf_op | source)
XLA Modules:
  0.0 180.9 jit_solution(12914678766459376052)
XLA Ops:
  1.7 3.0 %multiply_reduce_fusion.1 = (f32[128]{0:T(128)S(1)}, f32[128,1024]{1,0:T(8,128)S(1)}) fusion(bf16[128,2048]{1,0:T(8,128)(2,1)S(1)} %copy-done, bf16[2048,1024]{1,0:T(8,128)(2,1)} %param.14), kind=kOutput, calls=%fused_computation.50 | convolution fusion | flops 537395072 | bytes 5243392 | tf_op jit(solution)/shard_map/dot_general | solution.py:182
  6.6 3.1 %collective-permute-start = (bf16[136,512]{1,0:T(8,128)(2,1)S(1)}, bf16[136,512]{1,0:T(8,128)(2,1)S(1)}, u32[]{:S(2)}, u32[]{:S(2)}) collective-permute-start(bf16[136,512]{1,0:T(8,128)(2,1)S(1)} %get-tuple-element.3.refs_3_), channel_id=1, source_target_pairs={{0,2},{1,3},{2,0},{3,1},{4,6},{5,7},{6,4},{7,5},{8,10},{9,11},{10,... | collective-permute-start | bytes 417800 | tf_op jit(solution)/shard_map/ppermute | solution.py:131
  9.7 2.6 %collective-permute-start.1 = (bf16[136,512]{1,0:T(8,128)(2,1)S(1)}, bf16[136,512]{1,0:T(8,128)(2,1)S(1)}, u32[]{:S(2)}, u32[]{:S(2)}) collective-permute-start(bf16[136,512]{1,0:T(8,128)(2,1)S(1)} %get-tuple-element.3.refs_3_), channel_id=1, source_target_pairs={{0,4},{1,5},{2,6},{3,7},{4,0},{5,1},{6,2},{7,3},{8,12},{9,13},{10,... | collective-permute-start | bytes 417800 | tf_op jit(solution)/shard_map/ppermute | solution.py:131
  12.3 1.7 collective-permute-start.3
  14.0 1.5 collective-permute-start.7
  15.6 2.8 %fusion.37.refs_0_ = bf16[128,1024]{1,0:T(8,128)(2,1)} fusion(bf16[128,1024]{1,0:T(8,128)(2,1)S(1)} %multiply_convert_fusion.1, bf16[2,1024,1024]{2,1,0:T(8,128)(2,1)} %param.16), kind=kOutput, calls=%fused_computation.25 | convolution fusion | flops 268697600 | bytes 2621440 | tf_op jit(solution)/shard_map/dot_general | solution.py:195
  20.4 2.8 %collective-permute-done.1.refs_5_ = bf16[136,512]{1,0:T(8,128)(2,1)S(1)} collective-permute-done((bf16[136,512]{1,0:T(8,128)(2,1)S(1)}, bf16[136,512]{1,0:T(8,128)(2,1)S(1)}, u32[]{:S(2)}, u32[]{:S(2)}) %collective-permute-start.1) | collective-permute-done | bytes 139296 | tf_op jit(solution)/shard_map/ppermute | solution.py:131
  29.2 1.5 collective-permute-start.4
  31.2 1.5 collective-permute-start.6
  32.7 1.5 collective-permute-start.8
  35.6 1.5 collective-permute-start.9
  38.6 1.5 collective-permute-start.10
  41.2 1.5 collective-permute-start.11
  45.7 1.5 collective-permute-start.13
  81.5 2.7 %select_convert_fusion.refs_2_ = bf16[4096,128]{1,0:T(8,128)(2,1)} fusion(s32[4096]{0:T(1024)S(1)} %convert_element_type.68), kind=kLoop, calls=%fused_computation.11 | loop fusion | flops 1572864 | bytes 1064960 | tf_op jit(solution)/shard_map/convert_element_type | solution.py:150
  84.2 15.1 %attend.2 = bf16[128,1024]{1,0:T(8,128)(2,1)} custom-call(bf16[128,1024]{1,0:T(8,128)(2,1)} %fusion.37.refs_0_, bf16[128,128]{1,0:T(8,128)(2,1)} %fusion.54.refs_1_, bf16[4096,128]{1,0:T(8,128)(2,1)} %select_convert_fusion.refs_2_, bf16[136,512]{1,0:T(8,128)(2,1)} %copy-done.12, bf16[136,512]{1,0:T(8,128)(2,1)} %copy-done.3, bf16[136,512]{1,0:T(8,128)(2,1)} %copy-done.4, ...), custom_call_target="tpu_custom_call" | custom-call | flops 2147483648 | bytes 4194304 | tf_op jit(solution)/shard_map/attend/pallas_call | solution.py:112
  99.4 1.9 %multiply_reduce_fusion = (f32[128]{0:T(128)S(1)}, f32[128,1024]{1,0:T(8,128)S(1)}) fusion(f32[128,1024]{1,0:T(8,128)S(1)} %get-tuple-element.9, bf16[128,1024]{1,0:T(8,128)(2,1)} %attend.2, bf16[2,1024,1024]{2,1,0:T(8,128)(2,1)S(1)} %copy-done.1), kind=kOutput, calls=%fused_computation.46 | convolution fusion | flops 269090688 | bytes 3408384 | tf_op jit(solution)/shard_map/dot_general | solution.py:210
  101.9 2.2 %collective-permute-start.19 = (bf16[128,512]{1,0:T(8,128)(2,1)S(1)}, bf16[128,512]{1,0:T(8,128)(2,1)S(1)}, u32[]{:S(2)}, u32[]{:S(2)}) collective-permute-start(bf16[128,512]{1,0:T(8,128)(2,1)S(1)} %pad_maximum_fusion.9.refs_3_), channel_id=1, source_target_pairs={{0,2},{1,3},{2,0},{3,1},{4,6},{5,7},{6,4},{7,5},{8,10},{9,11},{10,... | collective-permute-start | bytes 393224 | tf_op jit(solution)/shard_map/ppermute | solution.py:131
  106.6 1.5 collective-permute-start.26
  108.1 1.5 collective-permute-start.22
  109.6 1.5 collective-permute-start.27
  111.1 5.9 %collective-permute-done.20.refs_5_ = bf16[128,512]{1,0:T(8,128)(2,1)S(1)} collective-permute-done((bf16[128,512]{1,0:T(8,128)(2,1)S(1)}, bf16[128,512]{1,0:T(8,128)(2,1)S(1)}, u32[]{:S(2)}, u32[]{:S(2)}) %collective-permute-start.20) | collective-permute-done | bytes 131104 | tf_op jit(solution)/shard_map/ppermute | solution.py:131
  119.1 1.5 collective-permute-start.28
  123.3 1.6 collective-permute-start.30
  126.1 1.6 collective-permute-start.31
  127.7 1.5 collective-permute-start.32
  132.7 1.5 collective-permute-done.33.refs_18_
  137.5 15.2 %attend.3 = bf16[128,1024]{1,0:T(8,128)(2,1)} custom-call(bf16[128,1024]{1,0:T(8,128)(2,1)} %fusion.34.refs_0_, bf16[128,128]{1,0:T(8,128)(2,1)} %fusion.54.refs_1_, bf16[4096,128]{1,0:T(8,128)(2,1)} %select_convert_fusion.refs_2_, bf16[128,512]{1,0:T(8,128)(2,1)} %copy-done.13, bf16[128,512]{1,0:T(8,128)(2,1)} %copy-done.14, bf16[128,512]{1,0:T(8,128)(2,1)} %copy-done.15, ...), custom_call_target="tpu_custom_call" | custom-call | flops 2147483648 | bytes 4194304 | tf_op jit(solution)/shard_map/attend/pallas_call | solution.py:112
  152.7 2.4 %convolution_convert_fusion = bf16[256,1024]{1,0:T(8,128)(2,1)S(1)} fusion(f32[128,1024]{1,0:T(8,128)S(1)} %get-tuple-element.11, bf16[128,1024]{1,0:T(8,128)(2,1)} %attend.3, bf16[2,1024,1024]{2,1,0:T(8,128)(2,1)} %param.19, s32[128]{0:T(128)S(1)} %copy-done.33, pred[128]{0:T(512)(128)(4,1)S(1)} %broadcast_compare_fusion), kind=kOutput, calls=%fused_computation.14 | convolution fusion | flops 336134144 | bytes 3408512 | tf_op jit(solution)/shard_map/dot_general | solution.py:213
  155.1 11.2 %all_to_all.11 = bf16[4,64,1024]{2,1,0:T(8,128)(2,1)S(1)} all-to-all(bf16[4,64,1024]{2,1,0:T(8,128)(2,1)S(1)} %bitcast.135), channel_id=1, replica_groups=mesh['grp'=4,'seq'=8] {'grp'}, dimensions={0} | all-to-all | bytes 1048576 | tf_op jit(solution)/shard_map/all_to_all | solution.py:215
  167.1 4.2 %all-to-all-start.1 = ((f32[8,1,1024]{2,1,0:T(1,128)}), f32[8,1,1024]{2,1,0:T(1,128)S(1)}, u32[]{:S(2)}, u32[]{:S(2)}) async-start(f32[8,1,1024]{2,1,0:T(1,128)} %broadcast_in_dim.20), calls=%async_computation.1 | async-start | bytes 65536 | tf_op jit(solution)/shard_map/all_to_all | solution.py:219
  171.3 6.7 %all-to-all-done.1 = f32[8,1,1024]{2,1,0:T(1,128)S(1)} async-done(((f32[8,1,1024]{2,1,0:T(1,128)}), f32[8,1,1024]{2,1,0:T(1,128)S(1)}, u32[]{:S(2)}, u32[]{:S(2)}) %all-to-all-start.1) | async-done | bytes 32800 | tf_op jit(solution)/shard_map/all_to_all | solution.py:219
  (219 shorter events, 71.1 us)
Async XLA Ops:
  6.6 13.8 %collective-permute-start = (bf16[136,512]{1,0:T(8,128)(2,1)S(1)}, bf16[136,512]{1,0:T(8,128)(2,1)S(1)}, u32[]{:S(2)}, u32[]{:S(2)}) collective-permute-start(bf16[136,512]{1,0:T(8,128)(2,1)S(1)} %get-tuple-element.3.refs_3_), channel_id=1, source_target_pairs={{0,2},{1,3},{2,0},{3,1},{4,6},{5,7},{6,4},{7,5},{8,10},{9,11},{10,... | collective-permute-start | bytes 417800 | tf_op jit(solution)/shard_map/ppermute | solution.py:131
  9.7 13.5 %collective-permute-start.1 = (bf16[136,512]{1,0:T(8,128)(2,1)S(1)}, bf16[136,512]{1,0:T(8,128)(2,1)S(1)}, u32[]{:S(2)}, u32[]{:S(2)}) collective-permute-start(bf16[136,512]{1,0:T(8,128)(2,1)S(1)} %get-tuple-element.3.refs_3_), channel_id=1, source_target_pairs={{0,4},{1,5},{2,6},{3,7},{4,0},{5,1},{6,2},{7,3},{8,12},{9,13},{10,... | collective-permute-start | bytes 417800 | tf_op jit(solution)/shard_map/ppermute | solution.py:131
  12.3 10.9 %collective-permute-start.2 = (bf16[136,512]{1,0:T(8,128)(2,1)S(1)}, bf16[136,512]{1,0:T(8,128)(2,1)S(1)}, u32[]{:S(2)}, u32[]{:S(2)}) collective-permute-start(bf16[136,512]{1,0:T(8,128)(2,1)S(1)} %get-tuple-element.3.refs_3_), channel_id=1, source_target_pairs={{0,6},{1,7},{2,4},{3,5},{4,2},{5,3},{6,0},{7,1},{8,14},{9,15},{10,... | collective-permute-start | bytes 417800 | tf_op jit(solution)/shard_map/ppermute | solution.py:131
  12.3 15.4 %collective-permute-start.3 = (bf16[136,512]{1,0:T(8,128)(2,1)S(1)}, bf16[136,512]{1,0:T(8,128)(2,1)S(1)}, u32[]{:S(2)}, u32[]{:S(2)}) collective-permute-start(bf16[136,512]{1,0:T(8,128)(2,1)S(1)} %get-tuple-element.3.refs_3_), channel_id=1, source_target_pairs={{0,16},{8,24},{16,0},{24,8},{1,17},{9,25},{17,1},{25,9},{2,18},{10... | collective-permute-start | bytes 417800 | tf_op jit(solution)/shard_map/ppermute | solution.py:131
  14.0 18.6 %collective-permute-start.7 = (bf16[136,512]{1,0:T(8,128)(2,1)S(1)}, bf16[136,512]{1,0:T(8,128)(2,1)S(1)}, u32[]{:S(2)}, u32[]{:S(2)}) collective-permute-start(bf16[136,512]{1,0:T(8,128)(2,1)S(1)} %get-tuple-element.3.refs_3_), channel_id=1, source_target_pairs={{0,1},{1,0},{2,3},{3,2},{4,5},{5,4},{6,7},{7,6},{8,9},{9,8},{10,11... | collective-permute-start | bytes 417800 | tf_op jit(solution)/shard_map/ppermute | solution.py:131
  23.3 49.1 %collective-permute-start.15 = (bf16[4,136,512]{2,1,0:T(8,128)(2,1)S(1)}, bf16[4,136,512]{2,1,0:T(8,128)(2,1)}, u32[]{:S(2)}, u32[]{:S(2)}) collective-permute-start(bf16[4,136,512]{2,1,0:T(8,128)(2,1)S(1)} %pad_maximum_fusion), channel_id=1, source_target_pairs={{0,8},{8,0},{16,24},{24,16},{1,9},{9,1},{17,25},{25,17},{2,10},{10... | collective-permute-start | bytes 1671176 | tf_op jit(solution)/shard_map/ppermute | solution.py:131
  29.2 6.5 %collective-permute-start.4 = (bf16[136,512]{1,0:T(8,128)(2,1)S(1)}, bf16[136,512]{1,0:T(8,128)(2,1)S(1)}, u32[]{:S(2)}, u32[]{:S(2)}) collective-permute-start(bf16[136,512]{1,0:T(8,128)(2,1)S(1)} %collective-permute-done.refs_4_), channel_id=1, source_target_pairs={{0,16},{8,24},{16,0},{24,8},{1,17},{9,25},{17,1},{25,9},{2,18},{10... | collective-permute-start | bytes 417800 | tf_op jit(solution)/shard_map/ppermute | solution.py:131
  30.6 8.0 %collective-permute-start.5 = (bf16[136,512]{1,0:T(8,128)(2,1)S(1)}, bf16[136,512]{1,0:T(8,128)(2,1)S(1)}, u32[]{:S(2)}, u32[]{:S(2)}) collective-permute-start(bf16[136,512]{1,0:T(8,128)(2,1)S(1)} %collective-permute-done.1.refs_5_), channel_id=1, source_target_pairs={{0,16},{8,24},{16,0},{24,8},{1,17},{9,25},{17,1},{25,9},{2,18},{10... | collective-permute-start | bytes 417800 | tf_op jit(solution)/shard_map/ppermute | solution.py:131
  31.2 10.0 %collective-permute-start.6 = (bf16[136,512]{1,0:T(8,128)(2,1)S(1)}, bf16[136,512]{1,0:T(8,128)(2,1)S(1)}, u32[]{:S(2)}, u32[]{:S(2)}) collective-permute-start(bf16[136,512]{1,0:T(8,128)(2,1)S(1)} %collective-permute-done.2.refs_6_), channel_id=1, source_target_pairs={{0,16},{8,24},{16,0},{24,8},{1,17},{9,25},{17,1},{25,9},{2,18},{10... | collective-permute-start | bytes 417800 | tf_op jit(solution)/shard_map/ppermute | solution.py:131
  32.7 10.7 %collective-permute-start.8 = (bf16[136,512]{1,0:T(8,128)(2,1)S(1)}, bf16[136,512]{1,0:T(8,128)(2,1)S(1)}, u32[]{:S(2)}, u32[]{:S(2)}) collective-permute-start(bf16[136,512]{1,0:T(8,128)(2,1)S(1)} %collective-permute-done.refs_4_), channel_id=1, source_target_pairs={{0,1},{1,0},{2,3},{3,2},{4,5},{5,4},{6,7},{7,6},{8,9},{9,8},{10,11... | collective-permute-start | bytes 417800 | tf_op jit(solution)/shard_map/ppermute | solution.py:131
  35.6 8.3 %collective-permute-start.9 = (bf16[136,512]{1,0:T(8,128)(2,1)S(1)}, bf16[136,512]{1,0:T(8,128)(2,1)}, u32[]{:S(2)}, u32[]{:S(2)}) collective-permute-start(bf16[136,512]{1,0:T(8,128)(2,1)S(1)} %collective-permute-done.1.refs_5_), channel_id=1, source_target_pairs={{0,1},{1,0},{2,3},{3,2},{4,5},{5,4},{6,7},{7,6},{8,9},{9,8},{10,11... | collective-permute-start | bytes 417800 | tf_op jit(solution)/shard_map/ppermute | solution.py:131
  38.6 7.1 %collective-permute-start.10 = (bf16[136,512]{1,0:T(8,128)(2,1)S(1)}, bf16[136,512]{1,0:T(8,128)(2,1)}, u32[]{:S(2)}, u32[]{:S(2)}) collective-permute-start(bf16[136,512]{1,0:T(8,128)(2,1)S(1)} %collective-permute-done.2.refs_6_), channel_id=1, source_target_pairs={{0,1},{1,0},{2,3},{3,2},{4,5},{5,4},{6,7},{7,6},{8,9},{9,8},{10,11... | collective-permute-start | bytes 417800 | tf_op jit(solution)/shard_map/ppermute | solution.py:131
  41.2 7.2 %collective-permute-start.11 = (bf16[136,512]{1,0:T(8,128)(2,1)S(1)}, bf16[136,512]{1,0:T(8,128)(2,1)}, u32[]{:S(2)}, u32[]{:S(2)}) collective-permute-start(bf16[136,512]{1,0:T(8,128)(2,1)S(1)} %collective-permute-done.7.refs_11_), channel_id=1, source_target_pairs={{0,16},{8,24},{16,0},{24,8},{1,17},{9,25},{17,1},{25,9},{2,18},{10... | collective-permute-start | bytes 417800 | tf_op jit(solution)/shard_map/ppermute | solution.py:131
  43.4 31.2 %collective-permute-start.16 = (bf16[4,136,512]{2,1,0:T(8,128)(2,1)S(1)}, bf16[4,136,512]{2,1,0:T(8,128)(2,1)}, u32[]{:S(2)}, u32[]{:S(2)}) collective-permute-start(bf16[4,136,512]{2,1,0:T(8,128)(2,1)S(1)} %pad_maximum_fusion.1), channel_id=1, source_target_pairs={{0,8},{8,0},{16,24},{24,16},{1,9},{9,1},{17,25},{25,17},{2,10},{10... | collective-permute-start | bytes 1671176 | tf_op jit(solution)/shard_map/ppermute | solution.py:131
  43.9 18.7 %collective-permute-start.12 = (bf16[136,512]{1,0:T(8,128)(2,1)S(1)}, bf16[136,512]{1,0:T(8,128)(2,1)}, u32[]{:S(2)}, u32[]{:S(2)}) collective-permute-start(bf16[136,512]{1,0:T(8,128)(2,1)S(1)} %collective-permute-done.8.refs_12_), channel_id=1, source_target_pairs={{0,16},{8,24},{16,0},{24,8},{1,17},{9,25},{17,1},{25,9},{2,18},{10... | collective-permute-start | bytes 417800 | tf_op jit(solution)/shard_map/ppermute | solution.py:131
  45.7 17.1 %collective-permute-start.13 = (bf16[136,512]{1,0:T(8,128)(2,1)S(1)}, bf16[136,512]{1,0:T(8,128)(2,1)}, u32[]{:S(2)}, u32[]{:S(2)}) collective-permute-start(bf16[136,512]{1,0:T(8,128)(2,1)S(1)} %collective-permute-done.5.refs_9_), channel_id=1, source_target_pairs={{0,1},{1,0},{2,3},{3,2},{4,5},{5,4},{6,7},{7,6},{8,9},{9,8},{10,11... | collective-permute-start | bytes 417800 | tf_op jit(solution)/shard_map/ppermute | solution.py:131
  48.4 14.3 %collective-permute-start.14 = (bf16[136,512]{1,0:T(8,128)(2,1)S(1)}, bf16[136,512]{1,0:T(8,128)(2,1)}, u32[]{:S(2)}, u32[]{:S(2)}) collective-permute-start(bf16[136,512]{1,0:T(8,128)(2,1)S(1)} %collective-permute-done.6.refs_10_), channel_id=1, source_target_pairs={{0,1},{1,0},{2,3},{3,2},{4,5},{5,4},{6,7},{7,6},{8,9},{9,8},{10,11... | collective-permute-start | bytes 417800 | tf_op jit(solution)/shard_map/ppermute | solution.py:131
  62.6 14.1 %collective-permute-start.17 = (bf16[4,136,512]{2,1,0:T(8,128)(2,1)S(1)}, bf16[4,136,512]{2,1,0:T(8,128)(2,1)}, u32[]{:S(2)}, u32[]{:S(2)}) collective-permute-start(bf16[4,136,512]{2,1,0:T(8,128)(2,1)S(1)} %pad_maximum_fusion.2), channel_id=1, source_target_pairs={{0,8},{8,0},{16,24},{24,16},{1,9},{9,1},{17,25},{25,17},{2,10},{10... | collective-permute-start | bytes 1671176 | tf_op jit(solution)/shard_map/ppermute | solution.py:131
  64.0 14.8 %collective-permute-start.18 = (bf16[4,136,512]{2,1,0:T(8,128)(2,1)S(1)}, bf16[4,136,512]{2,1,0:T(8,128)(2,1)}, u32[]{:S(2)}, u32[]{:S(2)}) collective-permute-start(bf16[4,136,512]{2,1,0:T(8,128)(2,1)S(1)} %pad_maximum_fusion.3), channel_id=1, source_target_pairs={{0,8},{8,0},{16,24},{24,16},{1,9},{9,1},{17,25},{25,17},{2,10},{10... | collective-permute-start | bytes 1671176 | tf_op jit(solution)/shard_map/ppermute | solution.py:131
  101.9 7.7 %collective-permute-start.19 = (bf16[128,512]{1,0:T(8,128)(2,1)S(1)}, bf16[128,512]{1,0:T(8,128)(2,1)S(1)}, u32[]{:S(2)}, u32[]{:S(2)}) collective-permute-start(bf16[128,512]{1,0:T(8,128)(2,1)S(1)} %pad_maximum_fusion.9.refs_3_), channel_id=1, source_target_pairs={{0,2},{1,3},{2,0},{3,1},{4,6},{5,7},{6,4},{7,5},{8,10},{9,11},{10,... | collective-permute-start | bytes 393224 | tf_op jit(solution)/shard_map/ppermute | solution.py:131
  104.1 12.9 %collective-permute-start.20 = (bf16[128,512]{1,0:T(8,128)(2,1)S(1)}, bf16[128,512]{1,0:T(8,128)(2,1)S(1)}, u32[]{:S(2)}, u32[]{:S(2)}) collective-permute-start(bf16[128,512]{1,0:T(8,128)(2,1)S(1)} %pad_maximum_fusion.9.refs_3_), channel_id=1, source_target_pairs={{0,4},{1,5},{2,6},{3,7},{4,0},{5,1},{6,2},{7,3},{8,12},{9,13},{10,... | collective-permute-start | bytes 393224 | tf_op jit(solution)/shard_map/ppermute | solution.py:131
  105.2 13.3 %collective-permute-start.21 = (bf16[128,512]{1,0:T(8,128)(2,1)S(1)}, bf16[128,512]{1,0:T(8,128)(2,1)S(1)}, u32[]{:S(2)}, u32[]{:S(2)}) collective-permute-start(bf16[128,512]{1,0:T(8,128)(2,1)S(1)} %pad_maximum_fusion.9.refs_3_), channel_id=1, source_target_pairs={{0,6},{1,7},{2,4},{3,5},{4,2},{5,3},{6,0},{7,1},{8,14},{9,15},{10,... | collective-permute-start | bytes 393224 | tf_op jit(solution)/shard_map/ppermute | solution.py:131
  106.6 12.5 %collective-permute-start.26 = (bf16[128,512]{1,0:T(8,128)(2,1)S(1)}, bf16[128,512]{1,0:T(8,128)(2,1)S(1)}, u32[]{:S(2)}, u32[]{:S(2)}) collective-permute-start(bf16[128,512]{1,0:T(8,128)(2,1)S(1)} %pad_maximum_fusion.9.refs_3_), channel_id=1, source_target_pairs={{0,1},{1,0},{2,3},{3,2},{4,5},{5,4},{6,7},{7,6},{8,9},{9,8},{10,11... | collective-permute-start | bytes 393224 | tf_op jit(solution)/shard_map/ppermute | solution.py:131
  108.1 12.5 %collective-permute-start.22 = (bf16[128,512]{1,0:T(8,128)(2,1)S(1)}, bf16[128,512]{1,0:T(8,128)(2,1)S(1)}, u32[]{:S(2)}, u32[]{:S(2)}) collective-permute-start(bf16[128,512]{1,0:T(8,128)(2,1)S(1)} %pad_maximum_fusion.9.refs_3_), channel_id=1, source_target_pairs={{0,16},{8,24},{16,0},{24,8},{1,17},{9,25},{17,1},{25,9},{2,18},{10... | collective-permute-start | bytes 393224 | tf_op jit(solution)/shard_map/ppermute | solution.py:131
  109.6 11.5 %collective-permute-start.27 = (bf16[128,512]{1,0:T(8,128)(2,1)S(1)}, bf16[128,512]{1,0:T(8,128)(2,1)S(1)}, u32[]{:S(2)}, u32[]{:S(2)}) collective-permute-start(bf16[128,512]{1,0:T(8,128)(2,1)S(1)} %collective-permute-done.19.refs_4_), channel_id=1, source_target_pairs={{0,1},{1,0},{2,3},{3,2},{4,5},{5,4},{6,7},{7,6},{8,9},{9,8},{10,11... | collective-permute-start | bytes 393224 | tf_op jit(solution)/shard_map/ppermute | solution.py:131
  117.0 6.3 %collective-permute-start.24 = (bf16[128,512]{1,0:T(8,128)(2,1)S(1)}, bf16[128,512]{1,0:T(8,128)(2,1)S(1)}, u32[]{:S(2)}, u32[]{:S(2)}) collective-permute-start(bf16[128,512]{1,0:T(8,128)(2,1)S(1)} %collective-permute-done.20.refs_5_), channel_id=1, source_target_pairs={{0,16},{8,24},{16,0},{24,8},{1,17},{9,25},{17,1},{25,9},{2,18},{10... | collective-permute-start | bytes 393224 | tf_op jit(solution)/shard_map/ppermute | solution.py:131
  118.5 7.6 %collective-permute-start.25 = (bf16[128,512]{1,0:T(8,128)(2,1)S(1)}, bf16[128,512]{1,0:T(8,128)(2,1)S(1)}, u32[]{:S(2)}, u32[]{:S(2)}) collective-permute-start(bf16[128,512]{1,0:T(8,128)(2,1)S(1)} %collective-permute-done.21.refs_6_), channel_id=1, source_target_pairs={{0,16},{8,24},{16,0},{24,8},{1,17},{9,25},{17,1},{25,9},{2,18},{10... | collective-permute-start | bytes 393224 | tf_op jit(solution)/shard_map/ppermute | solution.py:131
  119.1 8.6 %collective-permute-start.28 = (bf16[128,512]{1,0:T(8,128)(2,1)S(1)}, bf16[128,512]{1,0:T(8,128)(2,1)S(1)}, u32[]{:S(2)}, u32[]{:S(2)}) collective-permute-start(bf16[128,512]{1,0:T(8,128)(2,1)S(1)} %collective-permute-done.20.refs_5_), channel_id=1, source_target_pairs={{0,1},{1,0},{2,3},{3,2},{4,5},{5,4},{6,7},{7,6},{8,9},{9,8},{10,11... | collective-permute-start | bytes 393224 | tf_op jit(solution)/shard_map/ppermute | solution.py:131
  120.6 8.6 %collective-permute-start.29 = (bf16[128,512]{1,0:T(8,128)(2,1)S(1)}, bf16[128,512]{1,0:T(8,128)(2,1)S(1)}, u32[]{:S(2)}, u32[]{:S(2)}) collective-permute-start(bf16[128,512]{1,0:T(8,128)(2,1)S(1)} %collective-permute-done.21.refs_6_), channel_id=1, source_target_pairs={{0,1},{1,0},{2,3},{3,2},{4,5},{5,4},{6,7},{7,6},{8,9},{9,8},{10,11... | collective-permute-start | bytes 393224 | tf_op jit(solution)/shard_map/ppermute | solution.py:131
  121.1 8.7 %collective-permute-start.23 = (bf16[128,512]{1,0:T(8,128)(2,1)S(1)}, bf16[128,512]{1,0:T(8,128)(2,1)S(1)}, u32[]{:S(2)}, u32[]{:S(2)}) collective-permute-start(bf16[128,512]{1,0:T(8,128)(2,1)S(1)} %collective-permute-done.19.refs_4_), channel_id=1, source_target_pairs={{0,16},{8,24},{16,0},{24,8},{1,17},{9,25},{17,1},{25,9},{2,18},{10... | collective-permute-start | bytes 393224 | tf_op jit(solution)/shard_map/ppermute | solution.py:131
  123.3 6.7 %collective-permute-start.30 = (bf16[128,512]{1,0:T(8,128)(2,1)S(1)}, bf16[128,512]{1,0:T(8,128)(2,1)S(1)}, u32[]{:S(2)}, u32[]{:S(2)}) collective-permute-start(bf16[128,512]{1,0:T(8,128)(2,1)S(1)} %collective-permute-done.26.refs_11_), channel_id=1, source_target_pairs={{0,16},{8,24},{16,0},{24,8},{1,17},{9,25},{17,1},{25,9},{2,18},{10... | collective-permute-start | bytes 393224 | tf_op jit(solution)/shard_map/ppermute | solution.py:131
  167.1 10.9 %all-to-all-start.1 = ((f32[8,1,1024]{2,1,0:T(1,128)}), f32[8,1,1024]{2,1,0:T(1,128)S(1)}, u32[]{:S(2)}, u32[]{:S(2)}) async-start(f32[8,1,1024]{2,1,0:T(1,128)} %broadcast_in_dim.20), calls=%async_computation.1 | async-start | bytes 65536 | tf_op jit(solution)/shard_map/all_to_all | solution.py:219
  (52 other events, 816.7 us)

commit v2 on v1

--- a/solution.py
+++ b/solution.py
@@ -16,14 +16,18 @@
 FAR = -1e30
 
 
-def attend_kernel(stacked, carried, last, *refs):
+def attend_kernel(stacked, coded, carried, last, *refs):
     count = len(stacked)
-    q_ref, doc_ref, far_ref = refs[:3]
-    blocks = refs[3 : 3 + count]
-    refs = refs[3 + count :]
+    q_ref, doc_ref = refs[:2]
+    blocks = refs[2 : 2 + count]
+    refs = refs[2 + count :]
+    if not coded:
+        far_ref, refs = refs[0], refs[1:]
     if carried:
         acc_in, stat_in = refs[:2]
         refs = refs[2:]
+    if coded:
+        far_ref, refs = refs[0], refs[1:]
     if last:
         out_ref, ka, va = refs
     else:
@@ -31,6 +35,20 @@
     rows = q_ref.shape[0]
     lane = lax.broadcasted_iota(jnp.int32, (rows, LANES), 1)
     low = lane < HDIM
+    if coded:
+        at = 0
+        line = lax.broadcasted_iota(jnp.int32, (LANES, rows), 0).astype(jnp.float32)
+        same = (lax.broadcasted_iota(jnp.int32, (rows, rows), 0) == lax.broadcasted_iota(jnp.int32, (rows, rows), 1))
+        same = jnp.where(same, 1.0, 0.0).astype(jnp.bfloat16)
+        for block, number in zip(blocks, stacked):
+            for i in range(max(number, 1)):
+                view = block.at[i] if number else block
+                code = view[rows : rows + EXTRA, :rows].astype(jnp.float32)[:1]
+                across_keys = jnp.where(line == code, 0.0, FAR).astype(jnp.bfloat16)
+                far_ref[at : at + rows, :] = lax.dot_general(
+                    same, across_keys, (((1,), (1,)), ((), ())), preferred_element_type=jnp.float32
+                ).astype(jnp.bfloat16)
+                at += rows
     ka[:, LANES:] = far_ref[...]
     va[:, LANES:] = jnp.ones((va.shape[0], LANES), jnp.bfloat16)
     stats = jnp.zeros((rows, LANES), jnp.float32)
@@ -101,16 +119,18 @@
     rows, width = query.shape
     stacked = tuple(b.shape[0] if b.ndim == 3 else 0 for b in blocks)
     keys = rows * sum(max(n, 1) for n in stacked)
+    out = () if far is not None else (jax.ShapeDtypeStruct((keys, LANES), jnp.bfloat16),)
     if last:
-        out = jax.ShapeDtypeStruct((rows, width), jnp.bfloat16)
+        out = out + (jax.ShapeDtypeStruct((rows, width), jnp.bfloat16),)
     else:
-        out = (
+        out = out + (
             jax.ShapeDtypeStruct((rows, width), jnp.float32),
             jax.ShapeDtypeStruct((rows, LANES), jnp.float32),
         )
     carried = () if carry is None else carry
-    return pl.pallas_call(
-        functools.partial(attend_kernel, stacked, carry is not None, last),
+    given = () if far is None else (far,)
+    out = pl.pallas_call(
+        functools.partial(attend_kernel, stacked, far is None, carry is not None, last),
         out_shape=out,
         scratch_shapes=[
             pltpu.VMEM((keys, 2 * LANES), jnp.bfloat16),
@@ -123,7 +143,10 @@
             transcendentals=rows * keys * HEADS,
         ),
         name="attend",
-    )(query, doc, far, *blocks, *carried)
+    )(query, doc, *blocks, *given, *carried)
+    if far is None:
+        far, out = out[0], out[1:]
+    return far, out[0] if last else out
 
 
 def across(array, axis, bit):
@@ -146,8 +169,15 @@
     return [[b for g in groups for b in g] + other]
 
 
-def placement(code, lanes):
-    return jnp.where(code[:, None] == lanes[None, :], 0.0, FAR).astype(jnp.bfloat16)
+def route(packed, near):
+    groups = packed.shape[0]
+    if groups != 4:
+        return lax.all_to_all(packed, "grp", split_axis=0, concat_axis=0, tiled=True)
+    came = [packed[0]] + [across(packed[bit], "grp", bit) for bit in range(1, groups)]
+    flip = (near & 1) > 0
+    came = [jnp.where(flip, came[i ^ 1], came[i]) for i in range(groups)]
+    flip = (near & 2) > 0
+    return jnp.stack([jnp.where(flip, came[i ^ 2], came[i]) for i in range(groups)])
 
 
 def per_device(
@@ -171,16 +201,21 @@
     number = jnp.arange(rows, dtype=jnp.int32)
     earlier = (number[None, :] < number[:, None]) & (target[None, :] == target[:, None])
     rank = jnp.sum(earlier.astype(jnp.int32), axis=1)
-    slot_of = target * capacity + rank
+    near = lax.axis_index("grp") if groups == 4 else 0
+    slot_of = (target ^ near) * capacity + rank
     placing = (jnp.arange(slots, dtype=jnp.int32)[:, None] == slot_of[None, :]) & (
         span_mask[None, :] > 0
     )
     placing = placing.astype(jnp.bfloat16)
+    counted = (jnp.arange(groups, dtype=jnp.int32)[:, None] == target[None, :]) & (
+        span_mask[None, :] > 0
+    )
+    counted = counted.astype(jnp.bfloat16)
     lanes = jnp.arange(LANES, dtype=jnp.int32)
     doc = (target[:, None] == lanes[None, :]).astype(jnp.bfloat16)
     code = jnp.where(span_mask > 0, target, LANES).astype(jnp.bfloat16)
     states = jnp.dot(spans, w_in, preferred_element_type=jnp.float32).astype(jnp.bfloat16)
-    far = None
+    far = []
     for layer in range(w_query.shape[0]):
         xf = states.astype(jnp.float32)
         normed = (
@@ -197,28 +232,26 @@
         )
         query = query * jnp.bfloat16(HDIM**-0.5)
         stages = gather_blocks(block)
-        if far is None:
-            far = []
-            for stage in stages:
-                codes = [
-                    b[..., rows, :rows].reshape(-1) for b in stage
-                ]
-                far.append(placement(jnp.concatenate(codes).astype(jnp.int32), lanes))
         carry = None
         for i, stage in enumerate(stages):
-            carry = attend(query, doc, far[i], stage, carry, i == len(stages) - 1)
+            given = far[i] if layer else None
+            kept, carry = attend(query, doc, given, stage, carry, i == len(stages) - 1)
+            if not layer:
+                far.append(kept)
         states = (xf + jnp.dot(carry, w_out[layer], preferred_element_type=jnp.float32)).astype(
             jnp.bfloat16
         )
     packed = jnp.dot(placing, states, preferred_element_type=jnp.float32).astype(jnp.bfloat16)
     packed = packed.reshape(groups, capacity, states.shape[1])
-    hidden = lax.all_to_all(packed, "grp", split_axis=0, concat_axis=0, tiled=True)
+    parts = jnp.dot(counted, states, preferred_element_type=jnp.float32)
+    hidden = route(packed, near)
     hidden = hidden.reshape(slots, states.shape[1])
-    local_sum = jnp.sum(hidden.astype(jnp.float32), axis=0)
     size = lax.axis_size("seq")
     sums = lax.all_to_all(
-        jnp.broadcast_to(local_sum[None, :], (size, local_sum.shape[0])),
-        "seq",
+        jnp.broadcast_to(parts[:, None, :], (groups, size, parts.shape[1])).reshape(
+            groups * size, parts.shape[1]
+        ),
+        ("grp", "seq"),
         split_axis=0,
         concat_axis=0,
         tiled=True,

time: 182 us -> 130 us (0.71)
  local copies, waits for them, and re-layouts: 45.6 us -> 4.25 us
  blocking collectives: 11.2 us -> 0 us
  waiting for transfers between devices: 23.9 us -> 31.3 us
  other arithmetic: 8.39 us -> 3.3 us
    unnamed x110 -> x94, local copies, waits for them, and re-layouts: 30.2 us -> 3.38 us
    concatenate x16 -> x0, local copies, waits for them, and re-layouts: 11.3 us -> none  [per_device(): far.append(placement(jnp.concatenate(codes).astype(jnp.int32), lanes))]
    all_to_all x1 -> x0, blocking collectives: 11.2 us -> none  [per_device(): lax.all_to_all(packed, 'grp', split_axis=0, concat_axis=0, tiled=True)]
    ppermute x38 -> x41, waiting for transfers between devices: 17.2 us -> 25.3 us  [across(): return lax.ppermute(array, axis, [(i, i ^ bit) for i in range(size)])]
    convert_element_type x2 -> x0, other arithmetic: 3.39 us -> none  [the longest x1 2.68 us: placement(): jnp.where(code[:, None] == lanes[None, :], 0.0, FAR).astype(jnp.bfloat16)]
    slice x4 -> x1, local copies, waits for them, and re-layouts: 2.87 us -> 0.03 us  [route(): packed[bit]]
    dot_general x1, matrix products: 2.39 us -> 0.29 us  [per_device(): jnp.dot(placing, states, preferred_element_type=jnp.float32)]
    another operation x9, other arithmetic: 2.63 us -> 0.56 us  [gather_blocks(): other = [across(jnp.stack(g), 'grp', 1) for g in groups]]
  transfers between devices with their start and end apart: 39 -> 42, of which waited for: 12 -> 18; matrix products, arithmetic and copies ran while one was open for 26% -> 5% of each run, Pallas kernels for 0% -> 0%
where the time goes in v2:
time: 130 us
  starting transfers between devices  45.3 us (35%)
  waiting for transfers between devices  31.3 us (24%)
  Pallas kernels  30.8 us (24%)
  matrix products  12.7 us (10%)
  local copies, waits for them, and re-layouts  4.25 us (3%)
  other arithmetic  3.3 us (3%)
  between operations  2.07 us (2%)
    ppermute x41, starting transfers between devices, across(): return lax.ppermute(array, axis, [(i, i ^ bit) for i in range(size)])  40.6 us
    pallas_call x2, Pallas kernels, attend(): pl.pallas_call(functools.partial(attend_kernel, stacked, far is None, car...  30.8 us
    ppermute x41, waiting for transfers between devices, across(): return lax.ppermute(array, axis, [(i, i ^ bit) for i in range(size)])  25.3 us
    all_to_all x1, waiting for transfers between devices, per_device(): lax.all_to_all(jnp.broadcast_to(parts[:, None, :], (groups, size, parts.s...  6.03 us
    all_to_all x1, starting transfers between devices, per_device(): lax.all_to_all(jnp.broadcast_to(parts[:, None, :], (groups, size, parts.s...  4.69 us
    dot_general x2, matrix products, per_device(): jnp.dot(normed, w_query[layer], preferred_element_type=jnp.float32)  3.89 us
    dot_general x2, matrix products, per_device(): jnp.dot(carry, w_out[layer], preferred_element_type=jnp.float32)  3.76 us
    unnamed x94, local copies, waits for them, and re-layouts  3.38 us
  transfers between devices with their start and end apart: 42, of which 18 were waited for; matrix products, arithmetic and copies ran while one was open for 5% of the time, Pallas kernels for 0%

profile of v2, /device:TPU:0, one launch (start us, length us, event | category | flops | bytes accessed | tf_op | source)
XLA Modules:
  0.0 129.8 jit_solution(8489414966121217241)
XLA Ops:
  1.7 3.0 %multiply_reduce_fusion.1 = (f32[128]{0:T(128)S(1)}, f32[128,1024]{1,0:T(8,128)S(1)}) fusion(bf16[128,2048]{1,0:T(8,128)(2,1)S(1)} %copy-done, bf16[2048,1024]{1,0:T(8,128)(2,1)} %param.14), kind=kOutput, calls=%fused_computation.48 | convolution fusion | flops 537395072 | bytes 5243392 | tf_op jit(solution)/shard_map/dot_general | solution.py:217
  5.6 3.1 %collective-permute-start = (bf16[136,512]{1,0:T(8,128)(2,1)S(1)}, bf16[136,512]{1,0:T(8,128)(2,1)S(1)}, u32[]{:S(2)}, u32[]{:S(2)}) collective-permute-start(bf16[136,512]{1,0:T(8,128)(2,1)S(1)} %get-tuple-element.14.refs_2_), channel_id=1, source_target_pairs={{0,2},{1,3},{2,0},{3,1},{4,6},{5,7},{6,4},{7,5},{8,10},{9,11},{10,... | collective-permute-start | bytes 417800 | tf_op jit(solution)/shard_map/ppermute | solution.py:154
  8.7 2.6 %collective-permute-start.1 = (bf16[136,512]{1,0:T(8,128)(2,1)S(1)}, bf16[136,512]{1,0:T(8,128)(2,1)S(1)}, u32[]{:S(2)}, u32[]{:S(2)}) collective-permute-start(bf16[136,512]{1,0:T(8,128)(2,1)S(1)} %get-tuple-element.14.refs_2_), channel_id=1, source_target_pairs={{0,4},{1,5},{2,6},{3,7},{4,0},{5,1},{6,2},{7,3},{8,12},{9,13},{10,... | collective-permute-start | bytes 417800 | tf_op jit(solution)/shard_map/ppermute | solution.py:154
  11.3 1.7 %collective-permute-start.7 = (bf16[136,512]{1,0:T(8,128)(2,1)S(1)}, bf16[136,512]{1,0:T(8,128)(2,1)S(1)}, u32[]{:S(2)}, u32[]{:S(2)}) collective-permute-start(bf16[136,512]{1,0:T(8,128)(2,1)S(1)} %get-tuple-element.14.refs_2_), channel_id=1, source_target_pairs={{0,1},{1,0},{2,3},{3,2},{4,5},{5,4},{6,7},{7,6},{8,9},{9,8},{10,11... | collective-permute-start | bytes 417800 | tf_op jit(solution)/shard_map/ppermute | solution.py:154
  13.0 1.5 %collective-permute-start.3 = (bf16[136,512]{1,0:T(8,128)(2,1)S(1)}, bf16[136,512]{1,0:T(8,128)(2,1)S(1)}, u32[]{:S(2)}, u32[]{:S(2)}) collective-permute-start(bf16[136,512]{1,0:T(8,128)(2,1)S(1)} %get-tuple-element.14.refs_2_), channel_id=1, source_target_pairs={{0,16},{8,24},{16,0},{24,8},{1,17},{9,25},{17,1},{25,9},{2,18},{10... | collective-permute-start | bytes 417800 | tf_op jit(solution)/shard_map/ppermute | solution.py:154
  14.5 1.4 %collective-permute-start.8 = (bf16[136,512]{1,0:T(8,128)(2,1)S(1)}, bf16[136,512]{1,0:T(8,128)(2,1)S(1)}, u32[]{:S(2)}, u32[]{:S(2)}) collective-permute-start(bf16[136,512]{1,0:T(8,128)(2,1)S(1)} %collective-permute-done.refs_3_), channel_id=1, source_target_pairs={{0,1},{1,0},{2,3},{3,2},{4,5},{5,4},{6,7},{7,6},{8,9},{9,8},{10,11... | collective-permute-start | bytes 417800 | tf_op jit(solution)/shard_map/ppermute | solution.py:154
  15.9 6.3 %collective-permute-done.1.refs_4_ = bf16[136,512]{1,0:T(8,128)(2,1)S(1)} collective-permute-done((bf16[136,512]{1,0:T(8,128)(2,1)S(1)}, bf16[136,512]{1,0:T(8,128)(2,1)S(1)}, u32[]{:S(2)}, u32[]{:S(2)}) %collective-permute-start.1) | collective-permute-done | bytes 139296 | tf_op jit(solution)/shard_map/ppermute | solution.py:154
  22.2 1.5 %collective-permute-start.5 = (bf16[136,512]{1,0:T(8,128)(2,1)S(1)}, bf16[136,512]{1,0:T(8,128)(2,1)S(1)}, u32[]{:S(2)}, u32[]{:S(2)}) collective-permute-start(bf16[136,512]{1,0:T(8,128)(2,1)S(1)} %collective-permute-done.1.refs_4_), channel_id=1, source_target_pairs={{0,16},{8,24},{16,0},{24,8},{1,17},{9,25},{17,1},{25,9},{2,18},{10... | collective-permute-start | bytes 417800 | tf_op jit(solution)/shard_map/ppermute | solution.py:154
  24.2 1.5 %collective-permute-start.9 = (bf16[136,512]{1,0:T(8,128)(2,1)S(1)}, bf16[136,512]{1,0:T(8,128)(2,1)S(1)}, u32[]{:S(2)}, u32[]{:S(2)}) collective-permute-start(bf16[136,512]{1,0:T(8,128)(2,1)S(1)} %collective-permute-done.1.refs_4_), channel_id=1, source_target_pairs={{0,1},{1,0},{2,3},{3,2},{4,5},{5,4},{6,7},{7,6},{8,9},{9,8},{10,11... | collective-permute-start | bytes 417800 | tf_op jit(solution)/shard_map/ppermute | solution.py:154
  26.2 1.5 %collective-permute-start.4 = (bf16[136,512]{1,0:T(8,128)(2,1)S(1)}, bf16[136,512]{1,0:T(8,128)(2,1)S(1)}, u32[]{:S(2)}, u32[]{:S(2)}) collective-permute-start(bf16[136,512]{1,0:T(8,128)(2,1)S(1)} %collective-permute-done.refs_3_), channel_id=1, source_target_pairs={{0,16},{8,24},{16,0},{24,8},{1,17},{9,25},{17,1},{25,9},{2,18},{10... | collective-permute-start | bytes 417800 | tf_op jit(solution)/shard_map/ppermute | solution.py:154
  28.7 1.6 %collective-permute-start.11 = (bf16[136,512]{1,0:T(8,128)(2,1)S(1)}, bf16[136,512]{1,0:T(8,128)(2,1)S(1)}, u32[]{:S(2)}, u32[]{:S(2)}) collective-permute-start(bf16[136,512]{1,0:T(8,128)(2,1)S(1)} %collective-permute-done.7.refs_10_), channel_id=1, source_target_pairs={{0,16},{8,24},{16,0},{24,8},{1,17},{9,25},{17,1},{25,9},{2,18},{10... | collective-permute-start | bytes 417800 | tf_op jit(solution)/shard_map/ppermute | solution.py:154
  30.3 1.4 %collective-permute-done.6.refs_9_ = bf16[136,512]{1,0:T(8,128)(2,1)S(1)} collective-permute-done((bf16[136,512]{1,0:T(8,128)(2,1)S(1)}, bf16[136,512]{1,0:T(8,128)(2,1)S(1)}, u32[]{:S(2)}, u32[]{:S(2)}) %collective-permute-start.6) | collective-permute-done | bytes 139296 | tf_op jit(solution)/shard_map/ppermute | solution.py:154
  32.8 1.5 %collective-permute-start.13 = (bf16[136,512]{1,0:T(8,128)(2,1)S(1)}, bf16[136,512]{1,0:T(8,128)(2,1)S(1)}, u32[]{:S(2)}, u32[]{:S(2)}) collective-permute-start(bf16[136,512]{1,0:T(8,128)(2,1)S(1)} %collective-permute-done.5.refs_8_), channel_id=1, source_target_pairs={{0,1},{1,0},{2,3},{3,2},{4,5},{5,4},{6,7},{7,6},{8,9},{9,8},{10,11... | collective-permute-start | bytes 417800 | tf_op jit(solution)/shard_map/ppermute | solution.py:154
  37.9 1.5 %collective-permute-done.14.refs_17_ = bf16[136,512]{1,0:T(8,128)(2,1)S(1)} collective-permute-done((bf16[136,512]{1,0:T(8,128)(2,1)S(1)}, bf16[136,512]{1,0:T(8,128)(2,1)S(1)}, u32[]{:S(2)}, u32[]{:S(2)}) %collective-permute-start.14) | collective-permute-done | bytes 139296 | tf_op jit(solution)/shard_map/ppermute | solution.py:154
  43.4 15.5 %attend.2 = (bf16[4096,128]{1,0:T(8,128)(2,1)}, bf16[128,1024]{1,0:T(8,128)(2,1)}) custom-call(bf16[128,1024]{1,0:T(8,128)(2,1)} %fusion.37.refs_0_, bf16[128,128]{1,0:T(8,128)(2,1)} %fusion.52.refs_1_, bf16[136,512]{1,0:T(8,128)(2,1)} %copy-done.17, bf16[136,512]{1,0:T(8,128)(2,1)} %copy-done.2, bf16[136,512]{1,0:T(8,128)(2,1)} %copy-done.3, ...), custom_call_target="tpu_custom_call" | custom-call | flops 2147483648 | bytes 4194304 | tf_op jit(solution)/shard_map/attend/pallas_call | solution.py:132
  58.9 2.3 %multiply_reduce_fusion = (f32[128]{0:T(128)S(1)}, f32[128,1024]{1,0:T(8,128)S(1)}) fusion(f32[128,1024]{1,0:T(8,128)S(1)} %get-tuple-element.20, bf16[128,1024]{1,0:T(8,128)(2,1)} %get-tuple-element.4, bf16[2,1024,1024]{2,1,0:T(8,128)(2,1)} %param.19), kind=kOutput, calls=%fused_computation.44 | convolution fusion | flops 269090688 | bytes 3408384 | tf_op jit(solution)/shard_map/dot_general | solution.py:241
  61.9 3.2 %collective-permute-start.20 = (bf16[128,512]{1,0:T(8,128)(2,1)S(1)}, bf16[128,512]{1,0:T(8,128)(2,1)S(1)}, u32[]{:S(2)}, u32[]{:S(2)}) collective-permute-start(bf16[128,512]{1,0:T(8,128)(2,1)S(1)} %pad_maximum_fusion.10.refs_2_), channel_id=1, source_target_pairs={{0,4},{1,5},{2,6},{3,7},{4,0},{5,1},{6,2},{7,3},{8,12},{9,13},{10,... | collective-permute-start | bytes 393224 | tf_op jit(solution)/shard_map/ppermute | solution.py:154
  66.3 1.5 %collective-permute-start.26 = (bf16[128,512]{1,0:T(8,128)(2,1)S(1)}, bf16[128,512]{1,0:T(8,128)(2,1)S(1)}, u32[]{:S(2)}, u32[]{:S(2)}) collective-permute-start(bf16[128,512]{1,0:T(8,128)(2,1)S(1)} %pad_maximum_fusion.10.refs_2_), channel_id=1, source_target_pairs={{0,1},{1,0},{2,3},{3,2},{4,5},{5,4},{6,7},{7,6},{8,9},{9,8},{10,11... | collective-permute-start | bytes 393224 | tf_op jit(solution)/shard_map/ppermute | solution.py:154
  68.7 1.6 %collective-permute-done.19.refs_3_ = bf16[128,512]{1,0:T(8,128)(2,1)S(1)} collective-permute-done((bf16[128,512]{1,0:T(8,128)(2,1)S(1)}, bf16[128,512]{1,0:T(8,128)(2,1)S(1)}, u32[]{:S(2)}, u32[]{:S(2)}) %collective-permute-start.19) | collective-permute-done | bytes 131104 | tf_op jit(solution)/shard_map/ppermute | solution.py:154
  70.3 1.5 %collective-permute-start.27 = (bf16[128,512]{1,0:T(8,128)(2,1)S(1)}, bf16[128,512]{1,0:T(8,128)(2,1)S(1)}, u32[]{:S(2)}, u32[]{:S(2)}) collective-permute-start(bf16[128,512]{1,0:T(8,128)(2,1)S(1)} %collective-permute-done.19.refs_3_), channel_id=1, source_target_pairs={{0,1},{1,0},{2,3},{3,2},{4,5},{5,4},{6,7},{7,6},{8,9},{9,8},{10,11... | collective-permute-start | bytes 393224 | tf_op jit(solution)/shard_map/ppermute | solution.py:154
  71.8 3.2 %collective-permute-done.20.refs_4_ = bf16[128,512]{1,0:T(8,128)(2,1)S(1)} collective-permute-done((bf16[128,512]{1,0:T(8,128)(2,1)S(1)}, bf16[128,512]{1,0:T(8,128)(2,1)S(1)}, u32[]{:S(2)}, u32[]{:S(2)}) %collective-permute-start.20) | collective-permute-done | bytes 131104 | tf_op jit(solution)/shard_map/ppermute | solution.py:154
  77.1 1.5 %collective-permute-start.28 = (bf16[128,512]{1,0:T(8,128)(2,1)S(1)}, bf16[128,512]{1,0:T(8,128)(2,1)S(1)}, u32[]{:S(2)}, u32[]{:S(2)}) collective-permute-start(bf16[128,512]{1,0:T(8,128)(2,1)S(1)} %collective-permute-done.20.refs_4_), channel_id=1, source_target_pairs={{0,1},{1,0},{2,3},{3,2},{4,5},{5,4},{6,7},{7,6},{8,9},{9,8},{10,11... | collective-permute-start | bytes 393224 | tf_op jit(solution)/shard_map/ppermute | solution.py:154
  82.1 1.9 %collective-permute-done.25.refs_9_ = bf16[128,512]{1,0:T(8,128)(2,1)S(1)} collective-permute-done((bf16[128,512]{1,0:T(8,128)(2,1)S(1)}, bf16[128,512]{1,0:T(8,128)(2,1)S(1)}, u32[]{:S(2)}, u32[]{:S(2)}) %collective-permute-start.25) | collective-permute-done | bytes 131104 | tf_op jit(solution)/shard_map/ppermute | solution.py:154
  84.9 1.5 %collective-permute-start.32 = (bf16[128,512]{1,0:T(8,128)(2,1)S(1)}, bf16[128,512]{1,0:T(8,128)(2,1)S(1)}, u32[]{:S(2)}, u32[]{:S(2)}) collective-permute-start(bf16[128,512]{1,0:T(8,128)(2,1)S(1)} %collective-permute-done.24.refs_8_), channel_id=1, source_target_pairs={{0,1},{1,0},{2,3},{3,2},{4,5},{5,4},{6,7},{7,6},{8,9},{9,8},{10,11... | collective-permute-start | bytes 393224 | tf_op jit(solution)/shard_map/ppermute | solution.py:154
  88.4 1.4 %collective-permute-done.31.refs_15_ = bf16[128,512]{1,0:T(8,128)(2,1)S(1)} collective-permute-done((bf16[128,512]{1,0:T(8,128)(2,1)S(1)}, bf16[128,512]{1,0:T(8,128)(2,1)S(1)}, u32[]{:S(2)}, u32[]{:S(2)}) %collective-permute-start.31) | collective-permute-done | bytes 131104 | tf_op jit(solution)/shard_map/ppermute | solution.py:154
  89.9 1.5 %collective-permute-done.33.refs_17_ = bf16[128,512]{1,0:T(8,128)(2,1)S(1)} collective-permute-done((bf16[128,512]{1,0:T(8,128)(2,1)S(1)}, bf16[128,512]{1,0:T(8,128)(2,1)S(1)}, u32[]{:S(2)}, u32[]{:S(2)}) %collective-permute-start.33) | collective-permute-done | bytes 131104 | tf_op jit(solution)/shard_map/ppermute | solution.py:154
  92.1 2.7 %fusion.34.refs_0_ = bf16[128,1024]{1,0:T(8,128)(2,1)} fusion(bf16[128,1024]{1,0:T(8,128)(2,1)S(1)} %multiply_convert_fusion, bf16[2,1024,1024]{2,1,0:T(8,128)(2,1)} %param.16), kind=kOutput, calls=%fused_computation.22 | convolution fusion | flops 268697600 | bytes 2621440 | tf_op jit(solution)/shard_map/dot_general | solution.py:230
  94.9 15.3 %attend.3 = bf16[128,1024]{1,0:T(8,128)(2,1)} custom-call(bf16[128,1024]{1,0:T(8,128)(2,1)} %fusion.34.refs_0_, bf16[128,128]{1,0:T(8,128)(2,1)} %fusion.52.refs_1_, bf16[128,512]{1,0:T(8,128)(2,1)} %copy-done.18, bf16[128,512]{1,0:T(8,128)(2,1)} %copy-done.19, bf16[128,512]{1,0:T(8,128)(2,1)} %copy-done.20, bf16[128,512]{1,0:T(8,128)(2,1)} %copy-done.21, ...), custom_call_target="tpu_custom_call" | custom-call | flops 2147483648 | bytes 4194304 | tf_op jit(solution)/shard_map/attend/pallas_call | solution.py:132
  110.2 1.5 %fusion.24 = bf16[128,1024]{1,0:T(8,128)(2,1)S(1)} fusion(f32[128,1024]{1,0:T(8,128)S(1)} %get-tuple-element.22, bf16[128,1024]{1,0:T(8,128)(2,1)} %attend.3, bf16[2,1024,1024]{2,1,0:T(8,128)(2,1)S(1)} %copy-done.39), kind=kOutput, calls=%fused_computation.17 | convolution fusion | flops 268697600 | bytes 3145728 | tf_op jit(solution)/shard_map/dot_general | solution.py:241
  112.0 1.3 %collective-permute-start.38 = (bf16[64,1024]{1,0:T(8,128)(2,1)S(1)}, bf16[64,1024]{1,0:T(8,128)(2,1)S(1)}, u32[]{:S(2)}, u32[]{:S(2)}) collective-permute-start(bf16[64,1024]{1,0:T(8,128)(2,1)S(1)} %get-tuple-element.12), channel_id=1, source_target_pairs={{0,24},{8,16},{16,8},{24,0},{1,25},{9,17},{17,9},{25,1},{2,26},{10... | collective-permute-start | bytes 393224 | tf_op jit(solution)/shard_map/ppermute | solution.py:154
  115.2 4.7 %all-to-all-start = ((f32[32,1,1024]{2,1,0:T(1,128)}), f32[32,1,1024]{2,1,0:T(1,128)S(1)}, u32[]{:S(2)}, u32[]{:S(2)}) async-start(f32[32,1,1024]{2,1,0:T(1,128)} %all_to_all.6), calls=%async_computation | async-start | bytes 262144 | tf_op jit(solution)/shard_map/all_to_all | solution.py:250
  121.6 6.0 %all-to-all-done = f32[32,1,1024]{2,1,0:T(1,128)S(1)} async-done(((f32[32,1,1024]{2,1,0:T(1,128)}), f32[32,1,1024]{2,1,0:T(1,128)S(1)}, u32[]{:S(2)}, u32[]{:S(2)}) %all-to-all-start) | async-done | bytes 131104 | tf_op jit(solution)/shard_map/all_to_all | solution.py:250
  (190 shorter events, 29.5 us)
Async XLA Ops:
  5.6 8.9 %collective-permute-start = (bf16[136,512]{1,0:T(8,128)(2,1)S(1)}, bf16[136,512]{1,0:T(8,128)(2,1)S(1)}, u32[]{:S(2)}, u32[]{:S(2)}) collective-permute-start(bf16[136,512]{1,0:T(8,128)(2,1)S(1)} %get-tuple-element.14.refs_2_), channel_id=1, source_target_pairs={{0,2},{1,3},{2,0},{3,1},{4,6},{5,7},{6,4},{7,5},{8,10},{9,11},{10,... | collective-permute-start | bytes 417800 | tf_op jit(solution)/shard_map/ppermute | solution.py:154
  8.7 13.5 %collective-permute-start.1 = (bf16[136,512]{1,0:T(8,128)(2,1)S(1)}, bf16[136,512]{1,0:T(8,128)(2,1)S(1)}, u32[]{:S(2)}, u32[]{:S(2)}) collective-permute-start(bf16[136,512]{1,0:T(8,128)(2,1)S(1)} %get-tuple-element.14.refs_2_), channel_id=1, source_target_pairs={{0,4},{1,5},{2,6},{3,7},{4,0},{5,1},{6,2},{7,3},{8,12},{9,13},{10,... | collective-permute-start | bytes 417800 | tf_op jit(solution)/shard_map/ppermute | solution.py:154
  11.3 12.4 %collective-permute-start.2 = (bf16[136,512]{1,0:T(8,128)(2,1)S(1)}, bf16[136,512]{1,0:T(8,128)(2,1)S(1)}, u32[]{:S(2)}, u32[]{:S(2)}) collective-permute-start(bf16[136,512]{1,0:T(8,128)(2,1)S(1)} %get-tuple-element.14.refs_2_), channel_id=1, source_target_pairs={{0,6},{1,7},{2,4},{3,5},{4,2},{5,3},{6,0},{7,1},{8,14},{9,15},{10,... | collective-permute-start | bytes 417800 | tf_op jit(solution)/shard_map/ppermute | solution.py:154
  11.3 12.9 %collective-permute-start.7 = (bf16[136,512]{1,0:T(8,128)(2,1)S(1)}, bf16[136,512]{1,0:T(8,128)(2,1)S(1)}, u32[]{:S(2)}, u32[]{:S(2)}) collective-permute-start(bf16[136,512]{1,0:T(8,128)(2,1)S(1)} %get-tuple-element.14.refs_2_), channel_id=1, source_target_pairs={{0,1},{1,0},{2,3},{3,2},{4,5},{5,4},{6,7},{7,6},{8,9},{9,8},{10,11... | collective-permute-start | bytes 417800 | tf_op jit(solution)/shard_map/ppermute | solution.py:154
  13.0 12.7 %collective-permute-start.3 = (bf16[136,512]{1,0:T(8,128)(2,1)S(1)}, bf16[136,512]{1,0:T(8,128)(2,1)S(1)}, u32[]{:S(2)}, u32[]{:S(2)}) collective-permute-start(bf16[136,512]{1,0:T(8,128)(2,1)S(1)} %get-tuple-element.14.refs_2_), channel_id=1, source_target_pairs={{0,16},{8,24},{16,0},{24,8},{1,17},{9,25},{17,1},{25,9},{2,18},{10... | collective-permute-start | bytes 417800 | tf_op jit(solution)/shard_map/ppermute | solution.py:154
  14.5 11.7 %collective-permute-start.8 = (bf16[136,512]{1,0:T(8,128)(2,1)S(1)}, bf16[136,512]{1,0:T(8,128)(2,1)S(1)}, u32[]{:S(2)}, u32[]{:S(2)}) collective-permute-start(bf16[136,512]{1,0:T(8,128)(2,1)S(1)} %collective-permute-done.refs_3_), channel_id=1, source_target_pairs={{0,1},{1,0},{2,3},{3,2},{4,5},{5,4},{6,7},{7,6},{8,9},{9,8},{10,11... | collective-permute-start | bytes 417800 | tf_op jit(solution)/shard_map/ppermute | solution.py:154
  22.2 6.5 %collective-permute-start.5 = (bf16[136,512]{1,0:T(8,128)(2,1)S(1)}, bf16[136,512]{1,0:T(8,128)(2,1)S(1)}, u32[]{:S(2)}, u32[]{:S(2)}) collective-permute-start(bf16[136,512]{1,0:T(8,128)(2,1)S(1)} %collective-permute-done.1.refs_4_), channel_id=1, source_target_pairs={{0,16},{8,24},{16,0},{24,8},{1,17},{9,25},{17,1},{25,9},{2,18},{10... | collective-permute-start | bytes 417800 | tf_op jit(solution)/shard_map/ppermute | solution.py:154
  23.7 8.0 %collective-permute-start.6 = (bf16[136,512]{1,0:T(8,128)(2,1)S(1)}, bf16[136,512]{1,0:T(8,128)(2,1)S(1)}, u32[]{:S(2)}, u32[]{:S(2)}) collective-permute-start(bf16[136,512]{1,0:T(8,128)(2,1)S(1)} %collective-permute-done.2.refs_5_), channel_id=1, source_target_pairs={{0,16},{8,24},{16,0},{24,8},{1,17},{9,25},{17,1},{25,9},{2,18},{10... | collective-permute-start | bytes 417800 | tf_op jit(solution)/shard_map/ppermute | solution.py:154
  24.2 8.6 %collective-permute-start.9 = (bf16[136,512]{1,0:T(8,128)(2,1)S(1)}, bf16[136,512]{1,0:T(8,128)(2,1)S(1)}, u32[]{:S(2)}, u32[]{:S(2)}) collective-permute-start(bf16[136,512]{1,0:T(8,128)(2,1)S(1)} %collective-permute-done.1.refs_4_), channel_id=1, source_target_pairs={{0,1},{1,0},{2,3},{3,2},{4,5},{5,4},{6,7},{7,6},{8,9},{9,8},{10,11... | collective-permute-start | bytes 417800 | tf_op jit(solution)/shard_map/ppermute | solution.py:154
  25.7 8.6 %collective-permute-start.10 = (bf16[136,512]{1,0:T(8,128)(2,1)S(1)}, bf16[136,512]{1,0:T(8,128)(2,1)S(1)}, u32[]{:S(2)}, u32[]{:S(2)}) collective-permute-start(bf16[136,512]{1,0:T(8,128)(2,1)S(1)} %collective-permute-done.2.refs_5_), channel_id=1, source_target_pairs={{0,1},{1,0},{2,3},{3,2},{4,5},{5,4},{6,7},{7,6},{8,9},{9,8},{10,11... | collective-permute-start | bytes 417800 | tf_op jit(solution)/shard_map/ppermute | solution.py:154
  26.2 8.7 %collective-permute-start.4 = (bf16[136,512]{1,0:T(8,128)(2,1)S(1)}, bf16[136,512]{1,0:T(8,128)(2,1)S(1)}, u32[]{:S(2)}, u32[]{:S(2)}) collective-permute-start(bf16[136,512]{1,0:T(8,128)(2,1)S(1)} %collective-permute-done.refs_3_), channel_id=1, source_target_pairs={{0,16},{8,24},{16,0},{24,8},{1,17},{9,25},{17,1},{25,9},{2,18},{10... | collective-permute-start | bytes 417800 | tf_op jit(solution)/shard_map/ppermute | solution.py:154
  28.7 6.6 %collective-permute-start.11 = (bf16[136,512]{1,0:T(8,128)(2,1)S(1)}, bf16[136,512]{1,0:T(8,128)(2,1)S(1)}, u32[]{:S(2)}, u32[]{:S(2)}) collective-permute-start(bf16[136,512]{1,0:T(8,128)(2,1)S(1)} %collective-permute-done.7.refs_10_), channel_id=1, source_target_pairs={{0,16},{8,24},{16,0},{24,8},{1,17},{9,25},{17,1},{25,9},{2,18},{10... | collective-permute-start | bytes 417800 | tf_op jit(solution)/shard_map/ppermute | solution.py:154
  35.0 6.5 %collective-permute-start.15 = (bf16[4,136,512]{2,1,0:T(8,128)(2,1)S(1)}, bf16[4,136,512]{2,1,0:T(8,128)(2,1)S(1)}, u32[]{:S(2)}, u32[]{:S(2)}) collective-permute-start(bf16[4,136,512]{2,1,0:T(8,128)(2,1)S(1)} %pad_maximum_fusion), channel_id=1, source_target_pairs={{0,8},{8,0},{16,24},{24,16},{1,9},{9,1},{17,25},{25,17},{2,10},{10... | collective-permute-start | bytes 1671176 | tf_op jit(solution)/shard_map/ppermute | solution.py:154
  35.3 6.1 %collective-permute-start.17 = (bf16[4,136,512]{2,1,0:T(8,128)(2,1)S(1)}, bf16[4,136,512]{2,1,0:T(8,128)(2,1)S(1)}, u32[]{:S(2)}, u32[]{:S(2)}) collective-permute-start(bf16[4,136,512]{2,1,0:T(8,128)(2,1)S(1)} %pad_maximum_fusion.2), channel_id=1, source_target_pairs={{0,8},{8,0},{16,24},{24,16},{1,9},{9,1},{17,25},{25,17},{2,10},{10... | collective-permute-start | bytes 1671176 | tf_op jit(solution)/shard_map/ppermute | solution.py:154
  61.9 8.5 %collective-permute-start.19 = (bf16[128,512]{1,0:T(8,128)(2,1)S(1)}, bf16[128,512]{1,0:T(8,128)(2,1)S(1)}, u32[]{:S(2)}, u32[]{:S(2)}) collective-permute-start(bf16[128,512]{1,0:T(8,128)(2,1)S(1)} %pad_maximum_fusion.10.refs_2_), channel_id=1, source_target_pairs={{0,2},{1,3},{2,0},{3,1},{4,6},{5,7},{6,4},{7,5},{8,10},{9,11},{10,... | collective-permute-start | bytes 393224 | tf_op jit(solution)/shard_map/ppermute | solution.py:154
  61.9 13.1 %collective-permute-start.20 = (bf16[128,512]{1,0:T(8,128)(2,1)S(1)}, bf16[128,512]{1,0:T(8,128)(2,1)S(1)}, u32[]{:S(2)}, u32[]{:S(2)}) collective-permute-start(bf16[128,512]{1,0:T(8,128)(2,1)S(1)} %pad_maximum_fusion.10.refs_2_), channel_id=1, source_target_pairs={{0,4},{1,5},{2,6},{3,7},{4,0},{5,1},{6,2},{7,3},{8,12},{9,13},{10,... | collective-permute-start | bytes 393224 | tf_op jit(solution)/shard_map/ppermute | solution.py:154
  65.1 11.0 %collective-permute-start.21 = (bf16[128,512]{1,0:T(8,128)(2,1)S(1)}, bf16[128,512]{1,0:T(8,128)(2,1)S(1)}, u32[]{:S(2)}, u32[]{:S(2)}) collective-permute-start(bf16[128,512]{1,0:T(8,128)(2,1)S(1)} %pad_maximum_fusion.10.refs_2_), channel_id=1, source_target_pairs={{0,6},{1,7},{2,4},{3,5},{4,2},{5,3},{6,0},{7,1},{8,14},{9,15},{10,... | collective-permute-start | bytes 393224 | tf_op jit(solution)/shard_map/ppermute | solution.py:154
  66.3 10.8 %collective-permute-start.26 = (bf16[128,512]{1,0:T(8,128)(2,1)S(1)}, bf16[128,512]{1,0:T(8,128)(2,1)S(1)}, u32[]{:S(2)}, u32[]{:S(2)}) collective-permute-start(bf16[128,512]{1,0:T(8,128)(2,1)S(1)} %pad_maximum_fusion.10.refs_2_), channel_id=1, source_target_pairs={{0,1},{1,0},{2,3},{3,2},{4,5},{5,4},{6,7},{7,6},{8,9},{9,8},{10,11... | collective-permute-start | bytes 393224 | tf_op jit(solution)/shard_map/ppermute | solution.py:154
  67.8 10.7 %collective-permute-start.22 = (bf16[128,512]{1,0:T(8,128)(2,1)S(1)}, bf16[128,512]{1,0:T(8,128)(2,1)S(1)}, u32[]{:S(2)}, u32[]{:S(2)}) collective-permute-start(bf16[128,512]{1,0:T(8,128)(2,1)S(1)} %pad_maximum_fusion.10.refs_2_), channel_id=1, source_target_pairs={{0,16},{8,24},{16,0},{24,8},{1,17},{9,25},{17,1},{25,9},{2,18},{10... | collective-permute-start | bytes 393224 | tf_op jit(solution)/shard_map/ppermute | solution.py:154
  70.3 8.8 %collective-permute-start.27 = (bf16[128,512]{1,0:T(8,128)(2,1)S(1)}, bf16[128,512]{1,0:T(8,128)(2,1)S(1)}, u32[]{:S(2)}, u32[]{:S(2)}) collective-permute-start(bf16[128,512]{1,0:T(8,128)(2,1)S(1)} %collective-permute-done.19.refs_3_), channel_id=1, source_target_pairs={{0,1},{1,0},{2,3},{3,2},{4,5},{5,4},{6,7},{7,6},{8,9},{9,8},{10,11... | collective-permute-start | bytes 393224 | tf_op jit(solution)/shard_map/ppermute | solution.py:154
  75.0 6.2 %collective-permute-start.24 = (bf16[128,512]{1,0:T(8,128)(2,1)S(1)}, bf16[128,512]{1,0:T(8,128)(2,1)S(1)}, u32[]{:S(2)}, u32[]{:S(2)}) collective-permute-start(bf16[128,512]{1,0:T(8,128)(2,1)S(1)} %collective-permute-done.20.refs_4_), channel_id=1, source_target_pairs={{0,16},{8,24},{16,0},{24,8},{1,17},{9,25},{17,1},{25,9},{2,18},{10... | collective-permute-start | bytes 393224 | tf_op jit(solution)/shard_map/ppermute | solution.py:154
  76.1 8.0 %collective-permute-start.25 = (bf16[128,512]{1,0:T(8,128)(2,1)S(1)}, bf16[128,512]{1,0:T(8,128)(2,1)S(1)}, u32[]{:S(2)}, u32[]{:S(2)}) collective-permute-start(bf16[128,512]{1,0:T(8,128)(2,1)S(1)} %collective-permute-done.21.refs_5_), channel_id=1, source_target_pairs={{0,16},{8,24},{16,0},{24,8},{1,17},{9,25},{17,1},{25,9},{2,18},{10... | collective-permute-start | bytes 393224 | tf_op jit(solution)/shard_map/ppermute | solution.py:154
  77.1 7.9 %collective-permute-start.28 = (bf16[128,512]{1,0:T(8,128)(2,1)S(1)}, bf16[128,512]{1,0:T(8,128)(2,1)S(1)}, u32[]{:S(2)}, u32[]{:S(2)}) collective-permute-start(bf16[128,512]{1,0:T(8,128)(2,1)S(1)} %collective-permute-done.20.refs_4_), channel_id=1, source_target_pairs={{0,1},{1,0},{2,3},{3,2},{4,5},{5,4},{6,7},{7,6},{8,9},{9,8},{10,11... | collective-permute-start | bytes 393224 | tf_op jit(solution)/shard_map/ppermute | solution.py:154
  78.6 7.9 %collective-permute-start.29 = (bf16[128,512]{1,0:T(8,128)(2,1)S(1)}, bf16[128,512]{1,0:T(8,128)(2,1)S(1)}, u32[]{:S(2)}, u32[]{:S(2)}) collective-permute-start(bf16[128,512]{1,0:T(8,128)(2,1)S(1)} %collective-permute-done.21.refs_5_), channel_id=1, source_target_pairs={{0,1},{1,0},{2,3},{3,2},{4,5},{5,4},{6,7},{7,6},{8,9},{9,8},{10,11... | collective-permute-start | bytes 393224 | tf_op jit(solution)/shard_map/ppermute | solution.py:154
  79.1 8.0 %collective-permute-start.23 = (bf16[128,512]{1,0:T(8,128)(2,1)S(1)}, bf16[128,512]{1,0:T(8,128)(2,1)S(1)}, u32[]{:S(2)}, u32[]{:S(2)}) collective-permute-start(bf16[128,512]{1,0:T(8,128)(2,1)S(1)} %collective-permute-done.19.refs_3_), channel_id=1, source_target_pairs={{0,16},{8,24},{16,0},{24,8},{1,17},{9,25},{17,1},{25,9},{2,18},{10... | collective-permute-start | bytes 393224 | tf_op jit(solution)/shard_map/ppermute | solution.py:154
  81.3 7.2 %collective-permute-start.30 = (bf16[128,512]{1,0:T(8,128)(2,1)S(1)}, bf16[128,512]{1,0:T(8,128)(2,1)S(1)}, u32[]{:S(2)}, u32[]{:S(2)}) collective-permute-start(bf16[128,512]{1,0:T(8,128)(2,1)S(1)} %collective-permute-done.26.refs_10_), channel_id=1, source_target_pairs={{0,16},{8,24},{16,0},{24,8},{1,17},{9,25},{17,1},{25,9},{2,18},{10... | collective-permute-start | bytes 393224 | tf_op jit(solution)/shard_map/ppermute | solution.py:154
  87.2 7.7 %collective-permute-start.34 = (bf16[4,128,512]{2,1,0:T(8,128)(2,1)S(1)}, bf16[4,128,512]{2,1,0:T(8,128)(2,1)}, u32[]{:S(2)}, u32[]{:S(2)}) collective-permute-start(bf16[4,128,512]{2,1,0:T(8,128)(2,1)S(1)} %pad_maximum_fusion.4), channel_id=1, source_target_pairs={{0,8},{8,0},{16,24},{24,16},{1,9},{9,1},{17,25},{25,17},{2,10},{10... | collective-permute-start | bytes 1572872 | tf_op jit(solution)/shard_map/ppermute | solution.py:154
  88.4 6.4 %collective-permute-start.36 = (bf16[4,128,512]{2,1,0:T(8,128)(2,1)S(1)}, bf16[4,128,512]{2,1,0:T(8,128)(2,1)}, u32[]{:S(2)}, u32[]{:S(2)}) collective-permute-start(bf16[4,128,512]{2,1,0:T(8,128)(2,1)S(1)} %pad_maximum_fusion.6), channel_id=1, source_target_pairs={{0,8},{8,0},{16,24},{24,16},{1,9},{9,1},{17,25},{25,17},{2,10},{10... | collective-permute-start | bytes 1572872 | tf_op jit(solution)/shard_map/ppermute | solution.py:154
  112.0 7.9 %collective-permute-start.38 = (bf16[64,1024]{1,0:T(8,128)(2,1)S(1)}, bf16[64,1024]{1,0:T(8,128)(2,1)S(1)}, u32[]{:S(2)}, u32[]{:S(2)}) collective-permute-start(bf16[64,1024]{1,0:T(8,128)(2,1)S(1)} %get-tuple-element.12), channel_id=1, source_target_pairs={{0,24},{8,16},{16,8},{24,0},{1,25},{9,17},{17,9},{25,1},{2,26},{10... | collective-permute-start | bytes 393224 | tf_op jit(solution)/shard_map/ppermute | solution.py:154
  113.3 7.3 %collective-permute-start.39 = (bf16[64,1024]{1,0:T(8,128)(2,1)S(1)}, bf16[64,1024]{1,0:T(8,128)(2,1)S(1)}, u32[]{:S(2)}, u32[]{:S(2)}) collective-permute-start(bf16[64,1024]{1,0:T(8,128)(2,1)S(1)} %get-tuple-element.11), channel_id=1, source_target_pairs={{0,16},{8,24},{16,0},{24,8},{1,17},{9,25},{17,1},{25,9},{2,18},{10... | collective-permute-start | bytes 393224 | tf_op jit(solution)/shard_map/ppermute | solution.py:154
  114.2 6.5 %collective-permute-start.40 = (bf16[64,1024]{1,0:T(8,128)(2,1)S(1)}, bf16[64,1024]{1,0:T(8,128)(2,1)S(1)}, u32[]{:S(2)}, u32[]{:S(2)}) collective-permute-start(bf16[64,1024]{1,0:T(8,128)(2,1)S(1)} %get-tuple-element.10), channel_id=1, source_target_pairs={{0,8},{8,0},{16,24},{24,16},{1,9},{9,1},{17,25},{25,17},{2,10},{10... | collective-permute-start | bytes 393224 | tf_op jit(solution)/shard_map/ppermute | solution.py:154
  115.2 12.4 %all-to-all-start = ((f32[32,1,1024]{2,1,0:T(1,128)}), f32[32,1,1024]{2,1,0:T(1,128)S(1)}, u32[]{:S(2)}, u32[]{:S(2)}) async-start(f32[32,1,1024]{2,1,0:T(1,128)} %all_to_all.6), calls=%async_computation | async-start | bytes 262144 | tf_op jit(solution)/shard_map/all_to_all | solution.py:250
  (57 other events, 518.7 us)
